TPU v7x, 32 devices: a whole 2x2x4 slice. The times are simulated.
32 devices in a mesh: tm: 8 (over z, y), space: 4 (over x, core).
Axes of the slice: x: 2, y: 2, z: 4, core: 2. Of those that a mesh axis runs over, the one named last changes fastest.
Arguments:
- video_in: bfloat16 [8, 256, 64, 128], P('tm', 'space'), may hold values from -6 to 6
- cotangent: bfloat16 [8, 256, 64, 128], P('tm', 'space'), may hold values from -6 to 6
- kernel_a: bfloat16 [3, 3, 3, 64, 64], replicated, may hold values from -0.15625 to 0.15625
- kernel_b: bfloat16 [3, 3, 3, 64, 64], replicated, may hold values from -0.15625 to 0.15625
- plane_kernel: bfloat16 [3, 3, 64, 64], replicated, may hold values from -0.25 to 0.25
- plane_head: bfloat16 [64], replicated, may hold values from -0.75 to 0.75
- time_kernel: bfloat16 [3, 64, 64], replicated, may hold values from -0.4375 to 0.4375
- time_mixer: bfloat16 [64, 64], replicated, may hold values from -12 to 12
- time_head: bfloat16 [64], replicated, may hold values from -0.75 to 0.75
- listed: int32 [8], replicated, may hold values from 0 to 7, as said below
Outputs:
- video: bfloat16 [8, 256, 64, 128], P('tm', 'space')
- input_grad: bfloat16 [8, 256, 64, 128], P('tm', 'space')
- plane_scores: float32 [8, 4, 64, 128], P('tm', 'space')
- time_scores: float32 [4, 32, 64], P('space', 'tm')
Inputs may be any that keep to these rules, and one draw needn't show every extreme that they name: `listed`: 8 distinct frame indices; the first is always frame 8 // 2, and frames 0 and 7 are always among the others, which stand in random order.
All inputs are finite; a program needn't handle non-finite values.
Results may differ from a plain program's by a relative error of at most 0.0053.
Values may be sent and summed in bfloat16 or wider, within the bound.
A program may use at most 128 MiB of HBM per device.

v0:
```python
import jax
import jax.numpy as jnp
from jax import lax
from jax.sharding import PartitionSpec as P

LISTED = 8


def padded_2(array, sides, width):
    for axis, dim in sides:
        size, length = (lax.axis_size(axis), array.shape[dim])
        up = [(i, (i + 1) % size) for i in range(size - 1)]
        down = [(j, i) for i, j in up]
        last = lax.slice_in_dim(array, length - width, length, axis=dim)
        initial = lax.slice_in_dim(array, 0, width, axis=dim)
        before = lax.ppermute(last, axis, up)
        after = lax.ppermute(initial, axis, down)
        array = jnp.concatenate([before, array, after], axis=dim)
    return array


def cube_conv(volume, kernel):
    padded = padded_2(volume, (("tm", 0), ("space", 1)), 1)
    return lax.conv_general_dilated(
        padded[None],
        kernel,
        (1, 1, 1),
        [(0, 0), (0, 0), (1, 1)],
        dimension_numbers=("NDHCW", "DHWIO", "NDHCW"),
        preferred_element_type=jnp.float32,
    )[0]


def flipped(kernel):
    return jnp.swapaxes(kernel[::-1, ::-1, ::-1], 3, 4)


def silu_slope(values):
    logistic = jax.nn.sigmoid(values)
    return logistic * (1.0 + values * (1.0 - logistic))


def plane_map(rimmed, kernel, head):
    conv_out = lax.conv_general_dilated(
        rimmed,
        kernel,
        (1, 1),
        [(0, 0), (1, 1)],
        dimension_numbers=("NHCW", "HWIO", "NHCW"),
        preferred_element_type=jnp.float32,
    )
    return jnp.einsum(
        "nhow,o->nhw",
        jax.nn.silu(conv_out),
        head.astype(jnp.float32),
        precision=lax.Precision.HIGHEST,
    )


def pool_pairs(volume):
    shaped = volume.astype(jnp.float32).reshape(
        volume.shape[0], volume.shape[1] // 2, 2, volume.shape[2], volume.shape[3] // 2, 2
    )
    return jnp.mean(shaped, axis=(2, 5)).astype(jnp.bfloat16)


def time_conv(rimmed, kernel):
    length = rimmed.shape[0] - 2
    total = jnp.zeros((length, rimmed.shape[1], kernel.shape[2], rimmed.shape[3]), jnp.float32)
    for offset in range(3):
        total = total + jnp.einsum(
            "thcw,co->thow",
            rimmed[offset : offset + length],
            kernel[offset],
            preferred_element_type=jnp.float32,
        )
    return total


def time_head_map(time_mean, mixer, head):
    mixed_units = jnp.einsum(
        "hcw,co->how", time_mean, mixer.astype(jnp.float32), precision=lax.Precision.HIGHEST
    )
    return jnp.einsum(
        "how,o->hw",
        jax.nn.silu(mixed_units),
        head.astype(jnp.float32),
        precision=lax.Precision.HIGHEST,
    )


def shards(
    video_in,
    cotangent,
    kernel_a,
    kernel_b,
    plane_kernel,
    plane_head,
    time_kernel,
    time_mixer,
    time_head,
    listed,
):
    float_in = video_in.astype(jnp.float32)
    hidden_in = jax.nn.silu(float_in).astype(jnp.bfloat16)
    pre_act = cube_conv(hidden_in, kernel_a)
    inner_act = jax.nn.silu(pre_act).astype(jnp.bfloat16)
    generated = (float_in + cube_conv(inner_act, kernel_b)).astype(jnp.bfloat16)
    grad_pre = (cube_conv(cotangent, flipped(kernel_b)) * silu_slope(pre_act)).astype(jnp.bfloat16)
    input_grad = (
        cotangent.astype(jnp.float32)
        + cube_conv(grad_pre, flipped(kernel_a)) * silu_slope(float_in)
    ).astype(jnp.bfloat16)
    frames_here = generated.shape[0]
    rows_here = generated.shape[1]
    tm_count = lax.axis_size("tm")
    groups = tm_count // LISTED
    quarter = rows_here // groups
    rimmed = padded_2(generated, (("space", 1),), 1)
    frame_scores = plane_map(rimmed, plane_kernel, plane_head)
    first_frame = lax.axis_index("tm") * frames_here
    select = (
        listed[:, None] == first_frame + jnp.arange(frames_here, dtype=jnp.int32)[None, :]
    ).astype(jnp.float32)
    picked = jnp.einsum("kf,fhw->khw", select, frame_scores, precision=lax.Precision.HIGHEST)
    picked = picked.reshape(tm_count, quarter, frame_scores.shape[2])
    plane_scores = lax.psum_scatter(picked, "tm", scatter_dimension=0, tiled=True)[:, None]
    total_frames = frames_here * tm_count
    moved_rows = lax.all_to_all(generated, "tm", split_axis=1, concat_axis=0, tiled=True)
    clip_time = pool_pairs(moved_rows)
    padded_clip = jnp.pad(clip_time, ((1, 1), (0, 0), (0, 0), (0, 0)))
    totals = jnp.sum(jax.nn.silu(time_conv(padded_clip, time_kernel)), axis=0)
    time_mean = totals / total_frames
    time_scores = time_head_map(time_mean, time_mixer, time_head)[None]
    return (generated, input_grad, plane_scores, time_scores)


def solution(mesh):
    return jax.shard_map(
        shards,
        mesh=mesh,
        in_specs=(
            P("tm", "space", None, None),
            P("tm", "space", None, None),
            P(),
            P(),
            P(),
            P(),
            P(),
            P(),
            P(),
            P(),
        ),
        out_specs=(
            P("tm", "space", None, None),
            P("tm", "space", None, None),
            P("tm", "space", None, None),
            P("space", "tm", None),
        ),
        check_vma=False,
    )
```

profile of v0, /device:TPU:0, one launch (start us, length us, event | category | flops | bytes accessed | tf_op | source)
XLA Modules:
  0.0 582.6 jit_solution(2372129652147209022)
XLA Ops:
  7.2 1.4 collective-permute-start.9
  8.6 6.5 %collective-permute-start.8 = (bf16[1,64,64,128]{3,2,1,0:T(8,128)(2,1)}, bf16[1,64,64,128]{3,2,1,0:T(8,128)(2,1)}, u32[]{:S(2)}, u32[]{:S(2)}) collective-permute-start(bf16[1,64,64,128]{3,2,1,0:T(8,128)(2,1)} %param.11), channel_id=1, source_target_pairs={{0,4},{4,8},{8,12},{12,16},{16,20},{20,24},{24,28},{1,5},{5,9},{9,... | collective-permute-start | bytes 3145736 | tf_op jit(solution)/shard_map/ppermute | solution.py:16
  15.1 2.7 fusion.48
  19.2 5.5 collective-permute-start
  24.7 4.7 copy.112
  29.4 7.1 %collective-permute-done.9 = bf16[1,64,64,128]{3,2,1,0:T(8,128)(2,1)} collective-permute-done((bf16[1,64,64,128]{3,2,1,0:T(8,128)(2,1)}, bf16[1,64,64,128]{3,2,1,0:T(8,128)(2,1)}, u32[]{:S(2)}, u32[]{:S(2)}) %collective-permute-start.9) | collective-permute-done | bytes 1048608 | tf_op jit(solution)/shard_map/ppermute | solution.py:17
  36.5 5.5 copy.113
  42.0 38.8 %collective-permute-done.8 = bf16[1,64,64,128]{3,2,1,0:T(8,128)(2,1)} collective-permute-done((bf16[1,64,64,128]{3,2,1,0:T(8,128)(2,1)}, bf16[1,64,64,128]{3,2,1,0:T(8,128)(2,1)}, u32[]{:S(2)}, u32[]{:S(2)}) %collective-permute-start.8) | collective-permute-done | bytes 1048608 | tf_op jit(solution)/shard_map/ppermute | solution.py:16
  80.9 5.4 copy.111
  86.3 3.7 pad_maximum_fusion
  90.0 5.8 %fusion.110 = (bf16[3,1,64,128]{1,2,3,0:T(8,128)(2,1)}, bf16[3,1,64,128]{1,2,3,0:T(8,128)(2,1)}) fusion(bf16[3,64,64,128]{1,2,3,0:T(8,128)(2,1)S(1)} %pad_maximum_fusion), kind=kLoop, calls=%fused_computation.134 | loop fusion | bytes 196608 | tf_op jit(solution)/shard_map/slice | solution.py:14
  95.8 8.6 %copy.115 = bf16[3,1,64,128]{3,2,1,0:T(8,128)(2,1)S(1)} copy(bf16[3,1,64,128]{1,2,3,0:T(8,128)(2,1)} %get-tuple-element.13) | data formatting | bytes 98304 | tf_op jit(solution)/shard_map/slice | solution.py:15
  105.7 8.6 %copy.114 = bf16[3,1,64,128]{3,2,1,0:T(8,128)(2,1)S(1)} copy(bf16[3,1,64,128]{1,2,3,0:T(8,128)(2,1)} %get-tuple-element.12) | data formatting | bytes 98304 | tf_op jit(solution)/shard_map/slice | solution.py:14
  114.4 3.0 collective-permute-start.10
  119.6 3.9 collective-permute-start.2
  123.5 9.8 %copy.117 = bf16[3,1,64,128]{1,2,3,0:T(8,128)(2,1)} copy(bf16[3,1,64,128]{3,2,1,0:T(8,128)(2,1)S(1)} %collective-permute-done.11) | data formatting | bytes 98304 | tf_op jit(solution)/shard_map/ppermute | solution.py:17
  133.3 9.7 %copy.116 = bf16[3,1,64,128]{1,2,3,0:T(8,128)(2,1)} copy(bf16[3,1,64,128]{3,2,1,0:T(8,128)(2,1)S(1)} %collective-permute-done.10) | data formatting | bytes 98304 | tf_op jit(solution)/shard_map/ppermute | solution.py:16
  143.0 10.0 %maximum_bitcast_fusion = bf16[3,66,64,1,128]{1,2,4,0,3:T(8,128)(2,1)S(1)} fusion(bf16[3,1,64,128]{1,2,3,0:T(8,128)(2,1)} %copy.117, bf16[1,64,64,128]{1,2,3,0:T(8,128)(2,1)} %copy.113, bf16[1,64,64,128]{1,2,3,0:T(8,128)(2,1)S(1)} %copy.112, bf16[1,64,64,128]{1,2,3,0:T(8,128)(2,1)} %copy.111, bf16[3,1,64,128]{1,2,3,0:T(8,128)(2,1)} %copy.116), kind=kLoop, calls=%fused_computation.30 | loop fusion | flops 16220160 | bytes 6488064 | tf_op jit(solution)/shard_map/broadcast_in_dim | solution.py:25
  153.1 4.6 pad.9
  157.6 11.8 %copy.119 = bf16[3,66,64,1,8,17]{2,4,5,1,0,3:T(8,128)(2,1)} copy(bf16[3,66,64,1,8,17]{1,2,5,4,0,3:T(8,128)(2,1)} %bitcast.137) | data formatting | bytes 6893568 | tf_op jit(solution)/shard_map/conv_general_dilated | solution.py:24
  170.9 19.3 %broadcast_select_fusion.1 = f32[1,64,8,17,64]{4,2,3,1,0:T(8,128)S(1)} fusion(pred[8,17]{0,1:T(8,128)(4,1)S(1)} %copy-done.10, bf16[3,3,3,64,64]{4,3,2,1,0:T(8,128)(2,1)S(1)} %copy-done.6, bf16[3,66,64,1,7,2]{2,4,5,1,0,3:T(8,128)(2,1)S(1)} %slice.77, bf16[3,66,64,1,8,17]{2,4,5,1,0,3:T(8,128)(2,1)} %copy.119), kind=kOutput, calls=%fused_computation.55 | convolution fusion | flops 1937299456 | bytes 6251144 | tf_op jit(solution)/shard_map/conv_general_dilated | solution.py:24
  191.0 2.6 slice.78
  193.6 4.8 copy.140
  198.3 3.5 maximum_bitcast_fusion.1
  201.8 8.6 %copy.142 = bf16[3,66,64,1,128]{1,2,4,0,3:T(8,128)(2,1)} copy(bf16[3,66,64,1,128]{4,2,1,0,3:T(8,128)(2,1)} %maximum_bitcast_fusion.1) | data formatting | bytes 6488064
  210.4 7.8 %pad.5.clone = bf16[3,66,64,1,136]{1,2,4,0,3:T(8,128)(2,1)} pad(bf16[3,66,64,1,128]{1,2,4,0,3:T(8,128)(2,1)} %copy.142, bf16[]{:T(256)} %constant.25.clone.1), padding=0_0x0_0x0_0x0_0x1_7 | pad | bytes 6690818 | tf_op jit(solution)/shard_map/broadcast_in_dim | solution.py:25
  218.2 11.8 %copy.103 = bf16[3,66,64,1,8,17]{2,4,5,1,0,3:T(8,128)(2,1)} copy(bf16[3,66,64,1,8,17]{1,2,5,4,0,3:T(8,128)(2,1)} %bitcast.138) | data formatting | bytes 6893568 | tf_op jit(solution)/shard_map/conv_general_dilated | solution.py:24
  231.4 11.2 %broadcast_select_fusion.3 = f32[1,64,8,17,64]{4,2,3,1,0:T(8,128)S(1)} fusion(pred[8,17]{0,1:T(8,128)(4,1)S(1)} %copy-done.10, bf16[3,3,3,64,64]{4,3,2,1,0:T(8,128)(2,1)S(1)} %copy-done, bf16[3,66,64,1,7,2]{2,4,5,1,0,3:T(8,128)(2,1)S(1)} %slice.71, bf16[3,66,64,1,8,17]{2,4,5,1,0,3:T(8,128)(2,1)} %copy.103), kind=kOutput, calls=%fused_computation.57 | convolution fusion | flops 1937299456 | bytes 6251144 | tf_op jit(solution)/shard_map/conv_general_dilated | solution.py:24
  243.5 2.6 slice.72
  246.0 4.8 copy.138
  250.8 3.3 fusion.55
  255.4 6.0 %collective-permute-start.12 = (bf16[1,64,64,128]{3,2,1,0:T(8,128)(2,1)S(1)}, bf16[1,64,64,128]{3,2,1,0:T(8,128)(2,1)}, u32[]{:S(2)}, u32[]{:S(2)}) collective-permute-start(bf16[1,64,64,128]{3,2,1,0:T(8,128)(2,1)S(1)} %get-tuple-element.20), channel_id=1, source_target_pairs={{0,4},{4,8},{8,12},{12,16},{16,20},{20,24},{24,28},{1,5},{5,9},{9,... | collective-permute-start | bytes 3145736 | tf_op jit(solution)/shard_map/ppermute | solution.py:16
  262.7 9.7 %collective-permute-start.4 = (bf16[1,64,64,128]{3,2,1,0:T(8,128)(2,1)S(1)}, bf16[1,64,64,128]{3,2,1,0:T(8,128)(2,1)}, u32[]{:S(2)}, u32[]{:S(2)}) collective-permute-start(bf16[1,64,64,128]{3,2,1,0:T(8,128)(2,1)S(1)} %get-tuple-element.21), channel_id=1, source_target_pairs={{0,4},{4,8},{8,12},{12,16},{16,20},{20,24},{24,28},{1,5},{5,9},{9,... | collective-permute-start | bytes 3145736 | tf_op jit(solution)/shard_map/ppermute | solution.py:16
  272.4 9.2 %collective-permute-done.13 = bf16[1,64,64,128]{3,2,1,0:T(8,128)(2,1)} collective-permute-done((bf16[1,64,64,128]{3,2,1,0:T(8,128)(2,1)S(1)}, bf16[1,64,64,128]{3,2,1,0:T(8,128)(2,1)}, u32[]{:S(2)}, u32[]{:S(2)}) %collective-permute-start.13) | collective-permute-done | bytes 1048608 | tf_op jit(solution)/shard_map/ppermute | solution.py:17
  281.6 46.6 %collective-permute-done.12 = bf16[1,64,64,128]{3,2,1,0:T(8,128)(2,1)} collective-permute-done((bf16[1,64,64,128]{3,2,1,0:T(8,128)(2,1)S(1)}, bf16[1,64,64,128]{3,2,1,0:T(8,128)(2,1)}, u32[]{:S(2)}, u32[]{:S(2)}) %collective-permute-start.12) | collective-permute-done | bytes 1048608 | tf_op jit(solution)/shard_map/ppermute | solution.py:16
  330.2 4.2 collective-permute-start.14
  334.4 16.2 %collective-permute-done.4 = bf16[1,64,64,128]{3,2,1,0:T(8,128)(2,1)} collective-permute-done((bf16[1,64,64,128]{3,2,1,0:T(8,128)(2,1)S(1)}, bf16[1,64,64,128]{3,2,1,0:T(8,128)(2,1)}, u32[]{:S(2)}, u32[]{:S(2)}) %collective-permute-start.4) | collective-permute-done | bytes 1048608 | tf_op jit(solution)/shard_map/ppermute | solution.py:16
  352.7 3.4 collective-permute-start.6
  356.2 3.5 maximum_bitcast_fusion.3
  359.7 8.4 %copy.144 = bf16[3,66,64,1,128]{1,2,4,0,3:T(8,128)(2,1)} copy(bf16[3,66,64,1,128]{4,2,1,0,3:T(8,128)(2,1)} %maximum_bitcast_fusion.3) | data formatting | bytes 6488064
  368.1 7.8 %pad.11.clone = bf16[3,66,64,1,136]{1,2,4,0,3:T(8,128)(2,1)} pad(bf16[3,66,64,1,128]{1,2,4,0,3:T(8,128)(2,1)} %copy.144, bf16[]{:T(256)} %constant.25.clone.1), padding=0_0x0_0x0_0x0_0x1_7 | pad | bytes 6690818 | tf_op jit(solution)/shard_map/broadcast_in_dim | solution.py:25
  375.9 11.8 %copy.124 = bf16[3,66,64,1,8,17]{2,4,5,1,0,3:T(8,128)(2,1)} copy(bf16[3,66,64,1,8,17]{1,2,5,4,0,3:T(8,128)(2,1)} %bitcast.139) | data formatting | bytes 6893568 | tf_op jit(solution)/shard_map/conv_general_dilated | solution.py:24
  389.1 19.3 %broadcast_select_fusion = f32[1,64,8,17,64]{4,2,3,1,0:T(8,128)S(1)} fusion(pred[8,17]{0,1:T(8,128)(4,1)S(1)} %copy-done.10, bf16[3,3,3,64,64]{4,3,2,1,0:T(8,128)(2,1)S(1)} %copy-done, bf16[3,66,64,1,7,2]{2,4,5,1,0,3:T(8,128)(2,1)S(1)} %slice.79, bf16[3,66,64,1,8,17]{2,4,5,1,0,3:T(8,128)(2,1)} %copy.124), kind=kOutput, calls=%fused_computation.54 | convolution fusion | flops 1937299456 | bytes 6251144 | tf_op jit(solution)/shard_map/conv_general_dilated | solution.py:24
  409.2 2.6 slice.80
  411.8 4.8 copy.141
  416.6 3.3 maximum_bitcast_fusion.2
  419.9 8.4 %copy.143 = bf16[3,66,64,1,128]{1,2,4,0,3:T(8,128)(2,1)} copy(bf16[3,66,64,1,128]{4,2,1,0,3:T(8,128)(2,1)} %maximum_bitcast_fusion.2) | data formatting | bytes 6488064
  428.4 7.8 %pad.7.clone = bf16[3,66,64,1,136]{1,2,4,0,3:T(8,128)(2,1)} pad(bf16[3,66,64,1,128]{1,2,4,0,3:T(8,128)(2,1)} %copy.143, bf16[]{:T(256)} %constant.25.clone.1), padding=0_0x0_0x0_0x0_0x1_7 | pad | bytes 6690818 | tf_op jit(solution)/shard_map/broadcast_in_dim | solution.py:25
  436.2 11.8 %copy.108 = bf16[3,66,64,1,8,17]{2,4,5,1,0,3:T(8,128)(2,1)} copy(bf16[3,66,64,1,8,17]{1,2,5,4,0,3:T(8,128)(2,1)} %bitcast.140) | data formatting | bytes 6893568 | tf_op jit(solution)/shard_map/conv_general_dilated | solution.py:24
  449.3 11.2 %broadcast_select_fusion.2 = f32[1,64,8,17,64]{4,2,3,1,0:T(8,128)S(1)} fusion(pred[8,17]{0,1:T(8,128)(4,1)S(1)} %copy-done.10, bf16[3,3,3,64,64]{4,3,2,1,0:T(8,128)(2,1)S(1)} %copy-done.6, bf16[3,66,64,1,7,2]{2,4,5,1,0,3:T(8,128)(2,1)S(1)} %slice.73, bf16[3,66,64,1,8,17]{2,4,5,1,0,3:T(8,128)(2,1)} %copy.108), kind=kOutput, calls=%fused_computation.56 | convolution fusion | flops 1937299456 | bytes 6251144 | tf_op jit(solution)/shard_map/conv_general_dilated | solution.py:24
  461.4 2.6 slice.74
  463.9 5.1 copy.139
  469.0 4.6 fusion.54
  475.6 4.3 collective-permute-start.16
  479.9 9.3 %all-to-all-start = ((bf16[1,64,64,128]{3,2,0,1:T(8,128)(2,1)}), bf16[1,64,64,128]{3,2,0,1:T(8,128)(2,1)}, u32[]{:S(2)}, u32[]{:S(2)}) async-start(bf16[1,64,64,128]{3,2,0,1:T(8,128)(2,1)} %bitcast.34), calls=%async_computation.1 | async-start | bytes 2097152 | tf_op jit(solution)/shard_map/all_to_all | solution.py:129
  490.6 3.0 copy.145
  493.7 2.3 pad.13.clone
  495.9 3.4 copy.129
  500.3 4.7 divide_multiply_fusion
  505.9 5.0 fusion.33
  511.8 4.6 all-to-all-done
  516.4 2.2 copy.132
  518.6 4.0 convert_reduce_fusion
  524.8 50.7 %reduce-scatter.2.cloned.1.call-done = f32[1,64,128]{2,1,0:T(8,128)} async-done(((f32[8,64,128]{2,1,0:T(8,128)}), f32[1,64,128]{2,1,0:T(8,128)}) %reduce-scatter.2.cloned.1.call-update) | async-done | bytes 32784 | tf_op jit(solution)/shard_map/reduce_scatter | solution.py:127
  (68 shorter events, 28.7 us)
Async XLA Ops:
  7.2 224.2 %copy-start = (bf16[3,3,3,64,64]{4,3,2,1,0:T(8,128)(2,1)S(1)}, bf16[3,3,3,64,64]{4,3,2,1,0:T(8,128)(2,1)}, u32[]{:S(2)}) copy-start(bf16[3,3,3,64,64]{4,3,2,1,0:T(8,128)(2,1)} %param.12) | copy-start | bytes 663556
  7.2 29.4 %collective-permute-start.9 = (bf16[1,64,64,128]{3,2,1,0:T(8,128)(2,1)}, bf16[1,64,64,128]{3,2,1,0:T(8,128)(2,1)}, u32[]{:S(2)}, u32[]{:S(2)}) collective-permute-start(bf16[1,64,64,128]{3,2,1,0:T(8,128)(2,1)} %param.11), channel_id=1, source_target_pairs={{4,0},{8,4},{12,8},{16,12},{20,16},{24,20},{28,24},{5,1},{9,5},{13... | collective-permute-start | bytes 3145736 | tf_op jit(solution)/shard_map/ppermute | solution.py:17
  8.6 72.3 %collective-permute-start.8 = (bf16[1,64,64,128]{3,2,1,0:T(8,128)(2,1)}, bf16[1,64,64,128]{3,2,1,0:T(8,128)(2,1)}, u32[]{:S(2)}, u32[]{:S(2)}) collective-permute-start(bf16[1,64,64,128]{3,2,1,0:T(8,128)(2,1)} %param.11), channel_id=1, source_target_pairs={{0,4},{4,8},{8,12},{12,16},{16,20},{20,24},{24,28},{1,5},{5,9},{9,... | collective-permute-start | bytes 3145736 | tf_op jit(solution)/shard_map/ppermute | solution.py:16
  17.9 99.5 %collective-permute-start.1 = (bf16[1,64,64,128]{3,2,1,0:T(8,128)(2,1)}, bf16[1,64,64,128]{3,2,1,0:T(8,128)(2,1)}, u32[]{:S(2)}, u32[]{:S(2)}) collective-permute-start(bf16[1,64,64,128]{3,2,1,0:T(8,128)(2,1)} %fusion.48), channel_id=1, source_target_pairs={{4,0},{8,4},{12,8},{16,12},{20,16},{24,20},{28,24},{5,1},{9,5},{13... | collective-permute-start | bytes 3145736 | tf_op jit(solution)/shard_map/ppermute | solution.py:17
  19.2 98.3 %collective-permute-start = (bf16[1,64,64,128]{3,2,1,0:T(8,128)(2,1)}, bf16[1,64,64,128]{3,2,1,0:T(8,128)(2,1)}, u32[]{:S(2)}, u32[]{:S(2)}) collective-permute-start(bf16[1,64,64,128]{3,2,1,0:T(8,128)(2,1)} %fusion.48), channel_id=1, source_target_pairs={{0,4},{4,8},{8,12},{12,16},{16,20},{20,24},{24,28},{1,5},{5,9},{9,... | collective-permute-start | bytes 3145736 | tf_op jit(solution)/shard_map/ppermute | solution.py:16
  104.4 19.0 %collective-permute-start.11 = (bf16[3,1,64,128]{3,2,1,0:T(8,128)(2,1)S(1)}, bf16[3,1,64,128]{3,2,1,0:T(8,128)(2,1)S(1)}, u32[]{:S(2)}, u32[]{:S(2)}) collective-permute-start(bf16[3,1,64,128]{3,2,1,0:T(8,128)(2,1)S(1)} %copy.115), channel_id=1, source_target_pairs={{1,0},{2,1},{3,2},{5,4},{6,5},{7,6},{9,8},{10,9},{11,10},{13,12},{... | collective-permute-start | bytes 147464 | tf_op jit(solution)/shard_map/ppermute | solution.py:17
  114.4 18.9 %collective-permute-start.10 = (bf16[3,1,64,128]{3,2,1,0:T(8,128)(2,1)S(1)}, bf16[3,1,64,128]{3,2,1,0:T(8,128)(2,1)S(1)}, u32[]{:S(2)}, u32[]{:S(2)}) collective-permute-start(bf16[3,1,64,128]{3,2,1,0:T(8,128)(2,1)S(1)} %copy.114), channel_id=1, source_target_pairs={{0,1},{1,2},{2,3},{4,5},{5,6},{6,7},{8,9},{9,10},{10,11},{12,13},{... | collective-permute-start | bytes 147464 | tf_op jit(solution)/shard_map/ppermute | solution.py:16
  118.3 80.1 %collective-permute-start.3 = (bf16[3,1,64,128]{3,2,1,0:T(8,128)(2,1)S(1)}, bf16[3,1,64,128]{3,2,1,0:T(8,128)(2,1)S(1)}, u32[]{:S(2)}, u32[]{:S(2)}) collective-permute-start(bf16[3,1,64,128]{3,2,1,0:T(8,128)(2,1)S(1)} %get-tuple-element.19), channel_id=1, source_target_pairs={{1,0},{2,1},{3,2},{5,4},{6,5},{7,6},{9,8},{10,9},{11,10},{13,12},{... | collective-permute-start | bytes 147464 | tf_op jit(solution)/shard_map/ppermute | solution.py:17
  119.6 78.8 %collective-permute-start.2 = (bf16[3,1,64,128]{3,2,1,0:T(8,128)(2,1)S(1)}, bf16[3,1,64,128]{3,2,1,0:T(8,128)(2,1)S(1)}, u32[]{:S(2)}, u32[]{:S(2)}) collective-permute-start(bf16[3,1,64,128]{3,2,1,0:T(8,128)(2,1)S(1)} %get-tuple-element.18), channel_id=1, source_target_pairs={{0,1},{1,2},{2,3},{4,5},{5,6},{6,7},{8,9},{9,10},{10,11},{12,13},{... | collective-permute-start | bytes 147464 | tf_op jit(solution)/shard_map/ppermute | solution.py:16
  157.6 13.2 %copy-start.6 = (bf16[3,3,3,64,64]{4,3,2,1,0:T(8,128)(2,1)S(1)}, bf16[3,3,3,64,64]{4,3,2,1,0:T(8,128)(2,1)}, u32[]{:S(2)}) copy-start(bf16[3,3,3,64,64]{4,3,2,1,0:T(8,128)(2,1)} %param.13) | copy-start | bytes 663556
  157.6 13.2 %copy-start.10 = (pred[8,17]{0,1:T(8,128)(4,1)S(1)}, pred[8,17]{0,1:T(8,128)(4,1)}, u32[]{:S(2)}) copy-start(pred[8,17]{0,1:T(8,128)(4,1)} %constant.51) | copy-start | bytes 412
  254.1 27.5 %collective-permute-start.13 = (bf16[1,64,64,128]{3,2,1,0:T(8,128)(2,1)S(1)}, bf16[1,64,64,128]{3,2,1,0:T(8,128)(2,1)}, u32[]{:S(2)}, u32[]{:S(2)}) collective-permute-start(bf16[1,64,64,128]{3,2,1,0:T(8,128)(2,1)S(1)} %get-tuple-element.20), channel_id=1, source_target_pairs={{4,0},{8,4},{12,8},{16,12},{20,16},{24,20},{28,24},{5,1},{9,5},{13... | collective-permute-start | bytes 3145736 | tf_op jit(solution)/shard_map/ppermute | solution.py:17
  255.4 72.7 %collective-permute-start.12 = (bf16[1,64,64,128]{3,2,1,0:T(8,128)(2,1)S(1)}, bf16[1,64,64,128]{3,2,1,0:T(8,128)(2,1)}, u32[]{:S(2)}, u32[]{:S(2)}) collective-permute-start(bf16[1,64,64,128]{3,2,1,0:T(8,128)(2,1)S(1)} %get-tuple-element.20), channel_id=1, source_target_pairs={{0,4},{4,8},{8,12},{12,16},{16,20},{20,24},{24,28},{1,5},{5,9},{9,... | collective-permute-start | bytes 3145736 | tf_op jit(solution)/shard_map/ppermute | solution.py:16
  261.4 73.0 %collective-permute-start.5 = (bf16[1,64,64,128]{3,2,1,0:T(8,128)(2,1)S(1)}, bf16[1,64,64,128]{3,2,1,0:T(8,128)(2,1)}, u32[]{:S(2)}, u32[]{:S(2)}) collective-permute-start(bf16[1,64,64,128]{3,2,1,0:T(8,128)(2,1)S(1)} %get-tuple-element.21), channel_id=1, source_target_pairs={{4,0},{8,4},{12,8},{16,12},{20,16},{24,20},{28,24},{5,1},{9,5},{13... | collective-permute-start | bytes 3145736 | tf_op jit(solution)/shard_map/ppermute | solution.py:17
  262.7 87.9 %collective-permute-start.4 = (bf16[1,64,64,128]{3,2,1,0:T(8,128)(2,1)S(1)}, bf16[1,64,64,128]{3,2,1,0:T(8,128)(2,1)}, u32[]{:S(2)}, u32[]{:S(2)}) collective-permute-start(bf16[1,64,64,128]{3,2,1,0:T(8,128)(2,1)S(1)} %get-tuple-element.21), channel_id=1, source_target_pairs={{0,4},{4,8},{8,12},{12,16},{16,20},{20,24},{24,28},{1,5},{5,9},{9,... | collective-permute-start | bytes 3145736 | tf_op jit(solution)/shard_map/ppermute | solution.py:16
  328.9 27.2 %collective-permute-start.15 = (bf16[3,1,64,128]{3,2,1,0:T(8,128)(2,1)S(1)}, bf16[3,1,64,128]{3,2,1,0:T(8,128)(2,1)S(1)}, u32[]{:S(2)}, u32[]{:S(2)}) collective-permute-start(bf16[3,1,64,128]{3,2,1,0:T(8,128)(2,1)S(1)} %get-tuple-element.15), channel_id=1, source_target_pairs={{1,0},{2,1},{3,2},{5,4},{6,5},{7,6},{9,8},{10,9},{11,10},{13,12},{... | collective-permute-start | bytes 147464 | tf_op jit(solution)/shard_map/ppermute | solution.py:17
  330.2 25.9 %collective-permute-start.14 = (bf16[3,1,64,128]{3,2,1,0:T(8,128)(2,1)S(1)}, bf16[3,1,64,128]{3,2,1,0:T(8,128)(2,1)S(1)}, u32[]{:S(2)}, u32[]{:S(2)}) collective-permute-start(bf16[3,1,64,128]{3,2,1,0:T(8,128)(2,1)S(1)} %get-tuple-element.14), channel_id=1, source_target_pairs={{0,1},{1,2},{2,3},{4,5},{5,6},{6,7},{8,9},{9,10},{10,11},{12,13},{... | collective-permute-start | bytes 147464 | tf_op jit(solution)/shard_map/ppermute | solution.py:16
  351.4 65.2 %collective-permute-start.7 = (bf16[3,1,64,128]{3,2,1,0:T(8,128)(2,1)S(1)}, bf16[3,1,64,128]{3,2,1,0:T(8,128)(2,1)S(1)}, u32[]{:S(2)}, u32[]{:S(2)}) collective-permute-start(bf16[3,1,64,128]{3,2,1,0:T(8,128)(2,1)S(1)} %get-tuple-element.17), channel_id=1, source_target_pairs={{1,0},{2,1},{3,2},{5,4},{6,5},{7,6},{9,8},{10,9},{11,10},{13,12},{... | collective-permute-start | bytes 147464 | tf_op jit(solution)/shard_map/ppermute | solution.py:17
  352.7 63.9 %collective-permute-start.6 = (bf16[3,1,64,128]{3,2,1,0:T(8,128)(2,1)S(1)}, bf16[3,1,64,128]{3,2,1,0:T(8,128)(2,1)S(1)}, u32[]{:S(2)}, u32[]{:S(2)}) collective-permute-start(bf16[3,1,64,128]{3,2,1,0:T(8,128)(2,1)S(1)} %get-tuple-element.16), channel_id=1, source_target_pairs={{0,1},{1,2},{2,3},{4,5},{5,6},{6,7},{8,9},{9,10},{10,11},{12,13},{... | collective-permute-start | bytes 147464 | tf_op jit(solution)/shard_map/ppermute | solution.py:16
  463.9 5.1 copy-start.2
  469.0 20.2 %copy-start.8 = (s32[8]{0:T(128)S(1)}, s32[8]{0:T(128)}, u32[]{:S(2)}) copy-start(s32[8]{0:T(128)} %param.19) | copy-start | bytes 100
  474.3 14.9 %collective-permute-start.17 = (bf16[1,1,64,128]{3,2,1,0:T(8,128)(2,1)S(1)}, bf16[1,1,64,128]{3,2,1,0:T(8,128)(2,1)S(1)}, u32[]{:S(2)}, u32[]{:S(2)}) collective-permute-start(bf16[1,1,64,128]{3,2,1,0:T(8,128)(2,1)S(1)} %get-tuple-element.23), channel_id=1, source_target_pairs={{1,0},{2,1},{3,2},{5,4},{6,5},{7,6},{9,8},{10,9},{11,10},{13,12},{... | collective-permute-start | bytes 49160 | tf_op jit(solution)/shard_map/ppermute | solution.py:17
  475.6 13.7 %collective-permute-start.16 = (bf16[1,1,64,128]{3,2,1,0:T(8,128)(2,1)S(1)}, bf16[1,1,64,128]{3,2,1,0:T(8,128)(2,1)S(1)}, u32[]{:S(2)}, u32[]{:S(2)}) collective-permute-start(bf16[1,1,64,128]{3,2,1,0:T(8,128)(2,1)S(1)} %get-tuple-element.22), channel_id=1, source_target_pairs={{0,1},{1,2},{2,3},{4,5},{5,6},{6,7},{8,9},{9,10},{10,11},{12,13},{... | collective-permute-start | bytes 49160 | tf_op jit(solution)/shard_map/ppermute | solution.py:16
  479.9 36.5 %all-to-all-start = ((bf16[1,64,64,128]{3,2,0,1:T(8,128)(2,1)}), bf16[1,64,64,128]{3,2,0,1:T(8,128)(2,1)}, u32[]{:S(2)}, u32[]{:S(2)}) async-start(bf16[1,64,64,128]{3,2,0,1:T(8,128)(2,1)} %bitcast.34), calls=%async_computation.1 | async-start | bytes 2097152 | tf_op jit(solution)/shard_map/all_to_all | solution.py:129
  489.2 86.3 %reduce-scatter.2.cloned.1.call-start = ((), (), s32[]{:S(2)}) async-start(), calls=%async_computation.2 | async-start | bytes 294912 | tf_op jit(solution)/shard_map/reduce_scatter | solution.py:127
  493.7 6.7 %copy-start.7 = (bf16[3,3,64,64]{3,2,1,0:T(8,128)(2,1)S(1)}, bf16[3,3,64,64]{3,2,1,0:T(8,128)(2,1)}, u32[]{:S(2)}) copy-start(bf16[3,3,64,64]{3,2,1,0:T(8,128)(2,1)} %param.14) | copy-start | bytes 221188
  505.0 0.9 copy-start.5
  510.9 11.7 %copy-start.3 = (bf16[3,64,64]{2,1,0:T(8,128)(2,1)S(1)}, bf16[3,64,64]{2,1,0:T(8,128)(2,1)}, u32[]{:S(2)}) copy-start(bf16[3,64,64]{2,1,0:T(8,128)(2,1)} %param.16) | copy-start | bytes 73732
  522.6 52.9 %copy-start.1 = (bf16[3,3,3,64,64]{4,3,2,1,0:T(8,128)(2,1)S(1)}, bf16[3,3,3,64,64]{4,3,2,1,0:T(8,128)(2,1)}, u32[]{:S(2)}) copy-start(bf16[3,3,3,64,64]{4,3,2,1,0:T(8,128)(2,1)} %param.12) | copy-start | bytes 663556
  522.9 0.8 copy-start.4
  522.9 1.0 copy-start.9
Sparse Core Ops, SparseCore 0:
  511.9 63.5 reduce-scatter.1
where the time goes:
time: 593 us; the launch traced here: 583 us
  local copies, waits for them, and re-layouts  211 us (36%)
  waiting for transfers between devices  173 us (29%)
  matrix products  72.6 us (12%)
  starting transfers between devices  67.6 us (11%)
  other arithmetic  43.3 us (7%)
  between operations  14.8 us (2%)
    ppermute x9, waiting for transfers between devices, padded_2(): before = lax.ppermute(last, axis, up)  102 us
    conv_general_dilated x16, local copies, waits for them, and re-layouts, cube_conv(): lax.conv_general_dilated(padded[None], kernel, (1, 1, 1), [(0, 0), (0, 0)...  66.3 us
    conv_general_dilated x4, matrix products, cube_conv(): lax.conv_general_dilated(padded[None], kernel, (1, 1, 1), [(0, 0), (0, 0)...  60.9 us
    unnamed x31, local copies, waits for them, and re-layouts  52.7 us
    reduce_scatter x1, waiting for transfers between devices, shards(): lax.psum_scatter(picked, 'tm', scatter_dimension=0, tiled=True)[:, None]  50.7 us
    ppermute x9, starting transfers between devices, padded_2(): before = lax.ppermute(last, axis, up)  46.5 us
    broadcast_in_dim x4, local copies, waits for them, and re-layouts, cube_conv(): padded[None]  28 us
    broadcast_in_dim x4, other arithmetic, cube_conv(): padded[None]  20.4 us
  transfers between devices with their start and end apart: 20, of which 7 were waited for; matrix products, arithmetic and copies ran while one was open for 37% of the time, Pallas kernels for 0%

commit v1 on v0

v1 whole, which is shorter than its diff:
```python
import functools

import jax
import jax.numpy as jnp
from jax import lax
from jax.experimental import pallas as pl
from jax.experimental.pallas import tpu as pltpu
from jax.sharding import PartitionSpec as P


LISTED = 8
F32 = jnp.float32
BF16 = jnp.bfloat16


def logistic(values):
    return 1.0 / (1.0 + jnp.exp(-values))


def slope_of(values):
    s = logistic(values)
    return s * (1.0 + values * (1.0 - s))


def store_shifted(wide_ref, t, row, values):
    channels, width = values.shape
    lane = lax.broadcasted_iota(jnp.int32, values.shape, 1)
    before = jnp.where(lane == 0, 0.0, pltpu.roll(values, 1, 1))
    after = jnp.where(lane == width - 1, 0.0, pltpu.roll(values, width - 1, 1))
    wide_ref[t, row, 0:channels] = before.astype(BF16)
    wide_ref[t, row, channels : 2 * channels] = values.astype(BF16)
    wide_ref[t, row, 2 * channels : 3 * channels] = after.astype(BF16)


def fill(wide_ref, main_ref, top_ref, bottom_ref, change):
    frames, rows = main_ref.shape[:2]

    def per_frame(t, _):
        store_shifted(wide_ref, t, 0, change(top_ref[t, 0].astype(F32)))
        store_shifted(wide_ref, t, rows + 1, change(bottom_ref[t, 0].astype(F32)))
        for row in range(rows):
            store_shifted(wide_ref, t, row + 1, change(main_ref[t, row].astype(F32)))
        return 0

    lax.fori_loop(0, frames, per_frame, 0)


def slab(wide_ref, t, row):
    depth = 3 * wide_ref.shape[2]
    width = wide_ref.shape[3]
    left = wide_ref[t, pl.ds(row, 3)].reshape(depth, width)
    right = wide_ref[t, pl.ds(row + 1, 3)].reshape(depth, width)
    return jnp.concatenate([left, right], axis=1)


def conv_loop(wide_ref, weight_ref, rows, emit):
    frames = wide_ref.shape[0]
    out = weight_ref.shape[0] // 3

    def product(t, row):
        return jnp.dot(weight_ref[...], slab(wide_ref, t, row), preferred_element_type=F32)

    def pair(i, _):
        row = 2 * i
        first = product(0, row)

        def step(t, carry):
            ready, early = carry
            z = product(t, row)
            emit(t - 1, row, ready + z[2 * out :])
            return early + z[out : 2 * out], z[:out]

        carry = (first[out : 2 * out], first[:out])
        if frames <= 8:
            for t in range(1, frames):
                carry = step(t, carry)
        else:
            carry = lax.fori_loop(1, frames, step, carry)
        emit(frames - 1, row, carry[0])
        return 0

    lax.fori_loop(0, rows // 2, pair, 0)


def each_row(emit_row, width):
    def emit(t, row, total):
        emit_row(t, row, total[:, :width])
        emit_row(t, row + 1, total[:, width:])

    return emit


def edges(out_ref, first_ref, last_ref):
    rows = out_ref.shape[1]
    first_ref[...] = out_ref[:, 0:1]
    last_ref[...] = out_ref[:, rows - 1 : rows]


def pre_kernel(main_ref, top_ref, bottom_ref, weight_ref, inner_ref, slope_ref, first_ref, last_ref, wide_ref):
    rows, width = main_ref.shape[1], main_ref.shape[3]
    fill(wide_ref, main_ref, top_ref, bottom_ref, lambda v: v * logistic(v))

    def emit(t, row, total):
        s = logistic(total)
        inner_ref[t, row] = (total * s).astype(BF16)
        slope_ref[t, row] = s * (1.0 + total * (1.0 - s))

    conv_loop(wide_ref, weight_ref, rows, each_row(emit, width))
    edges(inner_ref, first_ref, last_ref)


def grad_pre_kernel(main_ref, top_ref, bottom_ref, weight_ref, slope_ref, out_ref, first_ref, last_ref, wide_ref):
    rows, width = main_ref.shape[1], main_ref.shape[3]
    fill(wide_ref, main_ref, top_ref, bottom_ref, lambda v: v)

    def emit(t, row, total):
        out_ref[t, row] = (total * slope_ref[t, row]).astype(BF16)

    conv_loop(wide_ref, weight_ref, rows, each_row(emit, width))
    edges(out_ref, first_ref, last_ref)


def video_kernel(main_ref, top_ref, bottom_ref, weight_ref, in_ref, out_ref, first_ref, last_ref, wide_ref):
    rows, width = main_ref.shape[1], main_ref.shape[3]
    fill(wide_ref, main_ref, top_ref, bottom_ref, lambda v: v)

    def emit(t, row, total):
        out_ref[t, row] = (in_ref[t, row].astype(F32) + total).astype(BF16)

    conv_loop(wide_ref, weight_ref, rows, each_row(emit, width))
    edges(out_ref, first_ref, last_ref)


def input_grad_kernel(main_ref, top_ref, bottom_ref, weight_ref, in_ref, cot_ref, out_ref, wide_ref):
    rows, width = main_ref.shape[1], main_ref.shape[3]
    fill(wide_ref, main_ref, top_ref, bottom_ref, lambda v: v)

    def emit(t, row, total):
        gain = slope_of(in_ref[t, row].astype(F32))
        out_ref[t, row] = (cot_ref[t, row].astype(F32) + total * gain).astype(BF16)

    conv_loop(wide_ref, weight_ref, rows, each_row(emit, width))


def score_kernel(
    listed_ref,
    main_ref,
    top_ref,
    bottom_ref,
    plane_ref,
    plane_head_ref,
    pool_ref,
    time_ref,
    mixer_ref,
    time_head_ref,
    plane_out_ref,
    time_out_ref,
    wide_ref,
    pooled_ref,
):
    frames, rows, channels, width = main_ref.shape
    half = width // 2

    def per_listed(k, _):
        t = listed_ref[k]
        store_shifted(wide_ref, 0, 0, top_ref[t, 0].astype(F32))
        store_shifted(wide_ref, 0, rows + 1, bottom_ref[t, 0].astype(F32))
        for row in range(rows):
            store_shifted(wide_ref, 0, row + 1, main_ref[t, row].astype(F32))
        for row in range(0, rows, 2):
            g = jnp.dot(plane_ref[...], slab(wide_ref, 0, row), preferred_element_type=F32)
            scores = jnp.sum(g * logistic(g) * plane_head_ref[...], axis=0, keepdims=True)
            plane_out_ref[k, row : row + 1] = scores[:, :width]
            plane_out_ref[k, row + 1 : row + 2] = scores[:, width:]
        return 0

    lax.fori_loop(0, plane_out_ref.shape[0], per_listed, 0)

    def per_row(i, _):
        zero = jnp.zeros((channels, half), BF16)
        pooled_ref[0:channels] = zero
        pooled_ref[(frames + 1) * channels :] = zero
        for t in range(frames):
            both = jnp.concatenate([main_ref[t, 2 * i], main_ref[t, 2 * i + 1]], axis=1)
            mean = jnp.dot(both, pool_ref[...], preferred_element_type=F32)
            pooled_ref[(t + 1) * channels : (t + 2) * channels] = mean.astype(BF16)
        total = jnp.zeros((time_ref.shape[0], half), F32)
        for t in range(frames):
            q = jnp.dot(
                time_ref[...],
                pooled_ref[t * channels : (t + 3) * channels],
                preferred_element_type=F32,
            )
            total = total + q * logistic(q)
        mixed = jnp.dot(
            mixer_ref[...],
            total / frames,
            precision=lax.Precision.HIGHEST,
            preferred_element_type=F32,
        )
        time_out_ref[i] = jnp.sum(
            mixed * logistic(mixed) * time_head_ref[...], axis=0, keepdims=True
        )
        return 0

    lax.fori_loop(0, rows // 2, per_row, 0)


def call(kernel, outs, scratch, smem, *operands):
    return run(kernel, outs, scratch, smem, operands)


def run(kernel, outs, scratch, smem, operands):
    vmem = pl.BlockSpec(memory_space=pltpu.VMEM)
    specs = [pl.BlockSpec(memory_space=pltpu.SMEM)] * smem + [vmem] * (len(operands) - smem)
    return pl.pallas_call(
        kernel,
        out_shape=[jax.ShapeDtypeStruct(shape, dtype) for shape, dtype in outs],
        in_specs=specs,
        out_specs=[vmem] * len(outs),
        scratch_shapes=[pltpu.VMEM(shape, dtype) for shape, dtype in scratch],
        compiler_params=pltpu.CompilerParams(vmem_limit_bytes=56 * 1024 * 1024),
    )(*operands)


def forward_weight(kernel):
    a, b, e, c, o = kernel.shape
    return kernel.transpose(0, 4, 1, 2, 3).reshape(a * o, b * e * c)


def backward_weight(kernel):
    a, b, e, o, c = kernel.shape
    return kernel[::-1, ::-1, ::-1].transpose(0, 3, 1, 2, 4).reshape(a * o, b * e * c)


def from_neighbours(first, last):
    tiles, parts = lax.axis_size("space"), lax.axis_size("tm")
    order = [part * tiles + tile for tile in range(tiles) for part in range(parts)]
    up = list(zip(order[:-1], order[1:]))
    down = [(j, i) for i, j in up]
    names = ("tm", "space")
    return lax.ppermute(last, names, up), lax.ppermute(first, names, down)


def shards(
    video_in,
    cotangent,
    kernel_a,
    kernel_b,
    plane_kernel,
    plane_head,
    time_kernel,
    time_mixer,
    time_head,
    listed,
):
    to_rows = functools.partial(lax.all_to_all, axis_name="tm", split_axis=1, concat_axis=0, tiled=True)
    to_frames = functools.partial(lax.all_to_all, axis_name="tm", split_axis=0, concat_axis=1, tiled=True)
    tm_count = lax.axis_size("tm")

    v = to_rows(video_in)
    frames, rows, channels, width = v.shape
    v_halo = from_neighbours(v[:, :1], v[:, rows - 1 :])
    cot = to_rows(cotangent)
    cot_halo = from_neighbours(cot[:, :1], cot[:, rows - 1 :])

    block = (v.shape, BF16)
    edge = ((frames, 1, channels, width), BF16)
    wide = ((frames, rows + 2, 3 * channels, width), BF16)

    inner, slope, first, last = call(
        pre_kernel, [block, (v.shape, F32), edge, edge], [wide], 0, v, *v_halo, forward_weight(kernel_a)
    )
    inner_halo = from_neighbours(first, last)
    grad_pre, first, last = call(
        grad_pre_kernel, [block, edge, edge], [wide], 0, cot, *cot_halo, backward_weight(kernel_b), slope
    )
    grad_halo = from_neighbours(first, last)
    video_rows, first, last = call(
        video_kernel, [block, edge, edge], [wide], 0, inner, *inner_halo, forward_weight(kernel_b), v
    )
    video_halo = from_neighbours(first, last)
    video = to_frames(video_rows)
    (grad_rows,) = call(input_grad_kernel, [block], [wide], 0, grad_pre, *grad_halo, backward_weight(kernel_a), v, cot)
    input_grad = to_frames(grad_rows)

    column = jnp.arange(width, dtype=jnp.int32) // 2
    pool = (column[:, None] == jnp.arange(width // 2, dtype=jnp.int32)[None, :]).astype(BF16) * 0.25
    pool = jnp.concatenate([pool, pool], axis=0).astype(BF16)
    b, e, c, o = plane_kernel.shape
    plane_weight = plane_kernel.reshape(b * e * c, o).T
    time_weight = time_kernel.reshape(-1, time_kernel.shape[2]).T
    maps, time_scores = call(
        score_kernel,
        [((LISTED, rows, width), F32), ((rows // 2, 1, width // 2), F32)],
        [
            ((1, rows + 2, 3 * channels, width), BF16),
            (((frames + 2) * channels, width // 2), BF16),
        ],
        1,
        listed,
        video_rows,
        *video_halo,
        plane_weight,
        plane_head.astype(F32)[:, None],
        pool,
        time_weight,
        time_mixer.astype(F32).T,
        time_head.astype(F32)[:, None],
    )
    groups = tm_count // LISTED
    moved = lax.all_to_all(jnp.repeat(maps, groups, axis=0), "tm", split_axis=0, concat_axis=0, tiled=True)
    moved = moved.reshape(groups, tm_count * rows // groups, width)
    if groups > 1:
        mine = lax.rem(lax.axis_index("tm"), groups)
        moved = lax.dynamic_index_in_dim(moved, mine, 0, keepdims=True)
    plane_scores = moved[:, None]
    return (video, input_grad, plane_scores, time_scores.reshape(1, rows // 2, width // 2))


def solution(mesh):
    return jax.shard_map(
        shards,
        mesh=mesh,
        in_specs=(
            P("tm", "space", None, None),
            P("tm", "space", None, None),
            P(),
            P(),
            P(),
            P(),
            P(),
            P(),
            P(),
            P(),
        ),
        out_specs=(
            P("tm", "space", None, None),
            P("tm", "space", None, None),
            P("tm", "space", None, None),
            P("space", "tm", None),
        ),
        check_vma=False,
    )
```

time: 593 us -> 214 us (0.36); the launches traced: 583 us -> 213 us
  local copies, waits for them, and re-layouts: 211 us -> 17.4 us
  waiting for transfers between devices: 173 us -> 48.9 us
  matrix products: 72.6 us -> 0 us
  blocking collectives: 0 us -> 63.9 us
  other arithmetic: 43.3 us -> 1.34 us
  Pallas kernels: 0 us -> 38.8 us
  starting transfers between devices: 67.6 us -> 41.5 us
  between operations: 14.8 us -> 0.93 us
    ppermute x18 -> x10, waiting for transfers between devices: 118 us -> 3.7 us  [from_neighbours(): return (lax.ppermute(last, names, up), lax.ppermute(first, names, down))]
    conv_general_dilated x18 -> x0, local copies, waits for them, and re-layouts: 70.7 us -> none  [the longest x16 66.3 us: cube_conv(): lax.conv_general_dilated(padded[None], kernel, (1, 1, 1), [(0, 0), (0, 0)...]
    conv_general_dilated x5 -> x0, matrix products: 65.6 us -> none  [the longest x4 60.9 us: cube_conv(): lax.conv_general_dilated(padded[None], kernel, (1, 1, 1), [(0, 0), (0, 0)...]
    all_to_all x0 -> x2, blocking collectives: none -> 63.9 us  [the longest x1 33.1 us: shards(): v = to_rows(video_in)]
    reduce_scatter x1 -> x0, waiting for transfers between devices: 50.7 us -> none  [shards(): lax.psum_scatter(picked, 'tm', scatter_dimension=0, tiled=True)[:, None]]
    unnamed x31 -> x42, local copies, waits for them, and re-layouts: 52.7 us -> 6.64 us
    all_to_all x1 -> x3, waiting for transfers between devices: 4.59 us -> 45.2 us  [the longest x1 27.1 us: shards(): video = to_frames(video_rows)]
    pallas_call x0 -> x5, Pallas kernels: none -> 38.8 us  [run(): pl.pallas_call(kernel, out_shape=[jax.ShapeDtypeStruct(shape, dtype) for...]
  transfers between devices with their start and end apart: 20 -> 13, of which waited for: 7 -> 3; matrix products, arithmetic and copies ran while one was open for 37% -> 6% of each run, Pallas kernels for 0% -> 18%
where the time goes in v1:
time: 214 us; the launch traced here: 213 us
  blocking collectives  63.9 us (30%)
  waiting for transfers between devices  48.9 us (23%)
  starting transfers between devices  41.5 us (19%)
  Pallas kernels  38.8 us (18%)
  local copies, waits for them, and re-layouts  17.4 us (8%)
    pallas_call x5, Pallas kernels, run(): pl.pallas_call(kernel, out_shape=[jax.ShapeDtypeStruct(shape, dtype) for...  38.8 us
    all_to_all x1, blocking collectives, shards(): v = to_rows(video_in)  33.1 us
    all_to_all x1, blocking collectives, shards(): input_grad = to_frames(grad_rows)  30.8 us
    ppermute x10, starting transfers between devices, from_neighbours(): return (lax.ppermute(last, names, up), lax.ppermute(first, names, down))  27.7 us
    all_to_all x1, waiting for transfers between devices, shards(): video = to_frames(video_rows)  27.1 us
    all_to_all x1, waiting for transfers between devices, shards(): cot = to_rows(cotangent)  18.1 us
    unnamed x42, local copies, waits for them, and re-layouts  6.64 us
    all_to_all x1, starting transfers between devices, shards(): lax.all_to_all(jnp.repeat(maps, groups, axis=0), 'tm', split_axis=0, conc...  5.79 us
  transfers between devices with their start and end apart: 13, of which 3 were waited for; matrix products, arithmetic and copies ran while one was open for 6% of the time, Pallas kernels for 18%

profile of v1, /device:TPU:0, one launch (start us, length us, event | category | flops | bytes accessed | tf_op | source)
XLA Modules:
  0.0 212.7 jit_solution(15789001579227141468)
XLA Ops:
  0.6 33.1 %all_to_all.53 = bf16[1,64,64,128]{3,2,0,1:T(8,128)(2,1)S(1)} all-to-all(bf16[1,64,64,128]{3,2,0,1:T(8,128)(2,1)} %bitcast.37), channel_id=1, replica_groups=mesh['tm'=8,'space'=4] {'tm'}, dimensions={1} | all-to-all | bytes 2097152 | tf_op jit(solution)/shard_map/all_to_all | solution.py:261
  33.7 3.7 %all-to-all-start.2 = ((bf16[1,64,64,128]{3,2,0,1:T(8,128)(2,1)}), bf16[1,64,64,128]{3,2,0,1:T(8,128)(2,1)S(1)}, u32[]{:S(2)}, u32[]{:S(2)}) async-start(bf16[1,64,64,128]{3,2,0,1:T(8,128)(2,1)} %bitcast.38), calls=%async_computation.2 | async-start | bytes 2097152 | tf_op jit(solution)/shard_map/all_to_all | solution.py:264
  37.4 0.0 copy-start.2
  37.5 1.7 copy.33
  39.2 1.1 reshape.54.weight_ref
  40.3 0.0 copy-done.16
  40.3 0.1 copy.40
  40.4 0.1 fusion
  40.5 0.6 convert_bitcast_fusion.mixer_ref
  41.1 3.9 %collective-permute-start = (bf16[8,1,64,128]{3,2,1,0:T(8,128)(2,1)S(1)}, bf16[8,1,64,128]{3,2,1,0:T(8,128)(2,1)S(1)}, u32[]{:S(2)}, u32[]{:S(2)}) collective-permute-start(bf16[8,1,64,128]{3,2,1,0:T(8,128)(2,1)S(1)} %get-tuple-element.31), channel_id=1, source_target_pairs={{0,4},{4,8},{8,12},{12,16},{16,20},{20,24},{24,28},{28,1},{1,5},{5... | collective-permute-start | bytes 393224 | tf_op jit(solution)/shard_map/ppermute | solution.py:242
  45.0 1.3 collective-permute-start.1
  46.3 18.1 %all-to-all-done.2 = bf16[1,64,64,128]{3,2,0,1:T(8,128)(2,1)S(1)} async-done(((bf16[1,64,64,128]{3,2,0,1:T(8,128)(2,1)}), bf16[1,64,64,128]{3,2,0,1:T(8,128)(2,1)S(1)}, u32[]{:S(2)}, u32[]{:S(2)}) %all-to-all-start.2) | async-done | bytes 1048608 | tf_op jit(solution)/shard_map/all_to_all | solution.py:264
  64.4 4.6 %collective-permute-start.4 = (bf16[8,1,64,128]{3,2,1,0:T(8,128)(2,1)S(1)}, bf16[8,1,64,128]{3,2,1,0:T(8,128)(2,1)S(1)}, u32[]{:S(2)}, u32[]{:S(2)}) collective-permute-start(bf16[8,1,64,128]{3,2,1,0:T(8,128)(2,1)S(1)} %get-tuple-element.29), channel_id=1, source_target_pairs={{0,4},{4,8},{8,12},{12,16},{16,20},{20,24},{24,28},{28,1},{1,5},{5... | collective-permute-start | bytes 393224 | tf_op jit(solution)/shard_map/ppermute | solution.py:242
  69.0 1.3 collective-permute-start.5
  70.3 0.0 collective-permute-done.top_ref
  70.4 0.0 collective-permute-done.1.bottom_ref
  70.4 0.6 copy-done.11
  71.0 0.6 copy-done.12
  71.6 8.0 %shard_map.129 = (bf16[8,8,64,128]{3,2,1,0:T(8,128)(2,1)}, f32[8,8,64,128]{3,2,1,0:T(8,128)}, bf16[8,1,64,128]{3,2,1,0:T(8,128)(2,1)}, bf16[8,1,64,128]{3,2,1,0:T(8,128)(2,1)}) custom-call(bf16[8,8,64,128]{3,2,1,0:T(8,128)(2,1)} %bitcast.27, bf16[8,1,64,128]{3,2,1,0:T(8,128)(2,1)} %copy-done.11, bf16[8,1,64,128]{3,2,1,0:T(8,128)(2,1)} %copy-done.12, ...), custom_call_target="tpu_custom_call" | custom-call | tf_op jit(solution)/shard_map/pallas_call | solution.py:216
  79.7 4.5 %collective-permute-start.2 = (bf16[8,1,64,128]{3,2,1,0:T(8,128)(2,1)}, bf16[8,1,64,128]{3,2,1,0:T(8,128)(2,1)S(1)}, u32[]{:S(2)}, u32[]{:S(2)}) collective-permute-start(bf16[8,1,64,128]{3,2,1,0:T(8,128)(2,1)} %get-tuple-element.17), channel_id=1, source_target_pairs={{0,4},{4,8},{8,12},{12,16},{16,20},{20,24},{24,28},{28,1},{1,5},{5... | collective-permute-start | bytes 393224 | tf_op jit(solution)/shard_map/ppermute | solution.py:242
  84.2 1.3 collective-permute-start.3
  85.6 0.9 copy.34
  86.5 1.1 reshape.55.weight_ref
  87.6 0.0 collective-permute-done.2.top_ref
  87.6 3.7 %collective-permute-done.3.bottom_ref = bf16[8,1,64,128]{3,2,1,0:T(8,128)(2,1)S(1)} collective-permute-done((bf16[8,1,64,128]{3,2,1,0:T(8,128)(2,1)}, bf16[8,1,64,128]{3,2,1,0:T(8,128)(2,1)S(1)}, u32[]{:S(2)}, u32[]{:S(2)}) %collective-permute-start.3) | collective-permute-done | bytes 131104 | tf_op jit(solution)/shard_map/ppermute | solution.py:242
  91.3 0.6 copy-done.14
  91.9 7.1 %shard_map.130 = (bf16[8,8,64,128]{3,2,1,0:T(8,128)(2,1)}, bf16[8,1,64,128]{3,2,1,0:T(8,128)(2,1)}, bf16[8,1,64,128]{3,2,1,0:T(8,128)(2,1)}) custom-call(bf16[8,8,64,128]{3,2,1,0:T(8,128)(2,1)} %get-tuple-element.16.main_ref, bf16[8,1,64,128]{3,2,1,0:T(8,128)(2,1)} %copy-done.13, bf16[8,1,64,128]{3,2,1,0:T(8,128)(2,1)} %copy-done.14, ...), custom_call_target="tpu_custom_call" | custom-call | tf_op jit(solution)/shard_map/pallas_call | solution.py:216
  99.1 3.7 %collective-permute-start.8 = (bf16[8,1,64,128]{3,2,1,0:T(8,128)(2,1)}, bf16[8,1,64,128]{3,2,1,0:T(8,128)(2,1)S(1)}, u32[]{:S(2)}, u32[]{:S(2)}) collective-permute-start(bf16[8,1,64,128]{3,2,1,0:T(8,128)(2,1)} %get-tuple-element.24), channel_id=1, source_target_pairs={{0,4},{4,8},{8,12},{12,16},{16,20},{20,24},{24,28},{28,1},{1,5},{5... | collective-permute-start | bytes 393224 | tf_op jit(solution)/shard_map/ppermute | solution.py:242
  102.8 1.3 collective-permute-start.9
  104.1 0.4 copy.36
  104.5 0.0 copy-start.4
  104.5 1.1 reshape.56.weight_ref
  105.7 0.0 collective-permute-done.4.top_ref
  105.7 0.0 collective-permute-done.5.bottom_ref
  105.7 0.6 copy-done.5
  106.3 0.0 copy-done.6
  106.4 7.5 %shard_map.131 = (bf16[8,8,64,128]{3,2,1,0:T(8,128)(2,1)}, bf16[8,1,64,128]{3,2,1,0:T(8,128)(2,1)}, bf16[8,1,64,128]{3,2,1,0:T(8,128)(2,1)}) custom-call(bf16[8,8,64,128]{3,2,1,0:T(8,128)(2,1)} %bitcast.31, bf16[8,1,64,128]{3,2,1,0:T(8,128)(2,1)} %copy-done.5, bf16[8,1,64,128]{3,2,1,0:T(8,128)(2,1)} %copy-done.6, bf16[192,576]{1,0:T(8,128)(2,1)} %reshape.56.weight_ref, ...), custom_call_target="tpu_custom_call" | custom-call | tf_op jit(solution)/shard_map/pallas_call | solution.py:216
  113.9 4.5 %collective-permute-start.6 = (bf16[8,1,64,128]{3,2,1,0:T(8,128)(2,1)}, bf16[8,1,64,128]{3,2,1,0:T(8,128)(2,1)S(1)}, u32[]{:S(2)}, u32[]{:S(2)}) collective-permute-start(bf16[8,1,64,128]{3,2,1,0:T(8,128)(2,1)} %get-tuple-element.22), channel_id=1, source_target_pairs={{0,4},{4,8},{8,12},{12,16},{16,20},{20,24},{24,28},{28,1},{1,5},{5... | collective-permute-start | bytes 393224 | tf_op jit(solution)/shard_map/ppermute | solution.py:242
  118.5 1.3 collective-permute-start.7
  119.8 0.6 pad_maximum_fusion.pool_ref
  120.4 0.8 copy.38
  121.2 0.7 copy.41.plane_head_ref
  121.9 0.7 copy.42.time_head_ref
  122.6 0.7 copy.39
  123.3 0.0 collective-permute-done.8.top_ref
  123.3 0.0 collective-permute-done.9.bottom_ref
  123.3 0.6 copy-done.7
  123.9 0.0 copy-done.9
  124.0 8.4 %shard_map.133 = (f32[8,8,128]{2,1,0:T(8,128)}, f32[4,1,64]{2,1,0:T(1,128)}) custom-call(s32[8]{0:T(128)} %listed_ref.1, bf16[8,8,64,128]{3,2,1,0:T(8,128)(2,1)} %get-tuple-element.19.main_ref, bf16[8,1,64,128]{3,2,1,0:T(8,128)(2,1)} %copy-done.7, bf16[8,1,64,128]{3,2,1,0:T(8,128)(2,1)} %copy-done.9, bf16[64,576]{1,0:T(8,128)(2,1)} %bitcast.39, ...), custom_call_target="tpu_custom_call" | custom-call | tf_op jit(solution)/shard_map/pallas_call | solution.py:216
  132.4 5.8 %all-to-all-start.4 = ((f32[8,8,128]{2,1,0:T(8,128)}), f32[8,8,128]{2,1,0:T(8,128)S(1)}, u32[]{:S(2)}, u32[]{:S(2)}) async-start(f32[8,8,128]{2,1,0:T(8,128)} %get-tuple-element.26), calls=%async_computation.4 | async-start | bytes 65536 | tf_op jit(solution)/shard_map/all_to_all | solution.py:312
  138.2 0.4 copy.37
  138.6 1.1 reshape.57.weight_ref
  139.7 0.0 collective-permute-done.6.top_ref
  139.7 0.0 collective-permute-done.7.bottom_ref
  139.7 0.6 copy-done.8
  140.4 0.0 copy-done.10
  140.4 7.6 %shard_map.132 = bf16[8,8,64,128]{3,2,1,0:T(8,128)(2,1)} custom-call(bf16[8,8,64,128]{3,2,1,0:T(8,128)(2,1)} %get-tuple-element.21.main_ref, bf16[8,1,64,128]{3,2,1,0:T(8,128)(2,1)} %copy-done.8, bf16[8,1,64,128]{3,2,1,0:T(8,128)(2,1)} %copy-done.10, bf16[192,576]{1,0:T(8,128)(2,1)} %reshape.57.weight_ref, bf16[8,8,64,128]{3,2,1,0:T(8,128)(2,1)} %bitcast.29, ...), custom_call_target="tpu_custom_call" | custom-call | tf_op jit(solution)/shard_map/pallas_call | solution.py:216
  148.0 0.0 all-to-all-done.4
  148.0 30.8 %all_to_all.54 = bf16[8,8,64,128]{3,2,1,0:T(8,128)(2,1)S(1)} all-to-all(bf16[8,8,64,128]{3,2,1,0:T(8,128)(2,1)} %shard_map.132), channel_id=1, replica_groups=mesh['tm'=8,'space'=4] {'tm'}, dimensions={0} | all-to-all | bytes 2097152 | tf_op jit(solution)/shard_map/all_to_all | solution.py:285
  178.8 4.2 %all-to-all-start.1 = ((bf16[8,8,64,128]{3,2,1,0:T(8,128)(2,1)}), bf16[8,8,64,128]{3,2,1,0:T(8,128)(2,1)S(1)}, u32[]{:S(2)}, u32[]{:S(2)}) async-start(bf16[8,8,64,128]{3,2,1,0:T(8,128)(2,1)} %get-tuple-element.19.main_ref), calls=%async_computation.1 | async-start | bytes 2097152 | tf_op jit(solution)/shard_map/all_to_all | solution.py:283
  183.1 27.1 %all-to-all-done.1 = bf16[8,8,64,128]{3,2,1,0:T(8,128)(2,1)S(1)} async-done(((bf16[8,8,64,128]{3,2,1,0:T(8,128)(2,1)}), bf16[8,8,64,128]{3,2,1,0:T(8,128)(2,1)S(1)}, u32[]{:S(2)}, u32[]{:S(2)}) %all-to-all-start.1) | async-done | bytes 1048608 | tf_op jit(solution)/shard_map/all_to_all | solution.py:283
  210.2 1.0 copy.46
  211.1 1.0 copy.47
  212.1 0.6 copy.48
  (33 shorter events, 0.2 us)
Async XLA Ops:
  33.7 7.4 %copy-start = (bf16[1,64,64,128]{3,2,0,1:T(8,128)(2,1)}, bf16[1,64,64,128]{3,2,0,1:T(8,128)(2,1)S(1)}, u32[]{:S(2)}) copy-start(bf16[1,64,64,128]{3,2,0,1:T(8,128)(2,1)S(1)} %all_to_all.53) | copy-start | bytes 3145732
  33.7 6.5 %copy-start.16 = (bf16[64,64]{1,0:T(8,128)(2,1)S(1)}, bf16[64,64]{1,0:T(8,128)(2,1)}, u32[]{:S(2)}) copy-start(bf16[64,64]{1,0:T(8,128)(2,1)} %param.17) | copy-start | bytes 24580
  33.7 6.7 %copy-start.17 = (bf16[64]{0:T(256)(128)(2,1)S(1)}, bf16[64]{0:T(256)(128)(2,1)}, u32[]{:S(2)}) copy-start(bf16[64]{0:T(256)(128)(2,1)} %param.15) | copy-start | bytes 388
  33.7 30.7 %all-to-all-start.2 = ((bf16[1,64,64,128]{3,2,0,1:T(8,128)(2,1)}), bf16[1,64,64,128]{3,2,0,1:T(8,128)(2,1)S(1)}, u32[]{:S(2)}, u32[]{:S(2)}) async-start(bf16[1,64,64,128]{3,2,0,1:T(8,128)(2,1)} %bitcast.38), calls=%async_computation.2 | async-start | bytes 2097152 | tf_op jit(solution)/shard_map/all_to_all | solution.py:264
  37.4 48.1 %copy-start.18 = (bf16[64]{0:T(256)(128)(2,1)S(1)}, bf16[64]{0:T(256)(128)(2,1)}, u32[]{:S(2)}) copy-start(bf16[64]{0:T(256)(128)(2,1)} %param.18) | copy-start | bytes 388
  37.4 48.1 %copy-start.2 = (bf16[3,3,3,64,64]{4,3,2,1,0:T(8,128)(2,1)S(1)}, bf16[3,3,3,64,64]{4,3,2,1,0:T(8,128)(2,1)}, u32[]{:S(2)}) copy-start(bf16[3,3,3,64,64]{4,3,2,1,0:T(8,128)(2,1)} %param.13) | copy-start | bytes 663556
  41.1 29.2 %collective-permute-start = (bf16[8,1,64,128]{3,2,1,0:T(8,128)(2,1)S(1)}, bf16[8,1,64,128]{3,2,1,0:T(8,128)(2,1)S(1)}, u32[]{:S(2)}, u32[]{:S(2)}) collective-permute-start(bf16[8,1,64,128]{3,2,1,0:T(8,128)(2,1)S(1)} %get-tuple-element.31), channel_id=1, source_target_pairs={{0,4},{4,8},{8,12},{12,16},{16,20},{20,24},{24,28},{28,1},{1,5},{5... | collective-permute-start | bytes 393224 | tf_op jit(solution)/shard_map/ppermute | solution.py:242
  45.0 25.3 %collective-permute-start.1 = (bf16[8,1,64,128]{3,2,1,0:T(8,128)(2,1)S(1)}, bf16[8,1,64,128]{3,2,1,0:T(8,128)(2,1)S(1)}, u32[]{:S(2)}, u32[]{:S(2)}) collective-permute-start(bf16[8,1,64,128]{3,2,1,0:T(8,128)(2,1)S(1)} %get-tuple-element.30), channel_id=1, source_target_pairs={{4,0},{8,4},{12,8},{16,12},{20,16},{24,20},{28,24},{1,28},{5,1},{9... | collective-permute-start | bytes 393224 | tf_op jit(solution)/shard_map/ppermute | solution.py:242
  64.4 34.7 %copy-start.1 = (bf16[1,64,64,128]{3,2,0,1:T(8,128)(2,1)}, bf16[1,64,64,128]{3,2,0,1:T(8,128)(2,1)S(1)}, u32[]{:S(2)}) copy-start(bf16[1,64,64,128]{3,2,0,1:T(8,128)(2,1)S(1)} %all-to-all-done.2) | copy-start | bytes 3145732
  64.4 41.2 %collective-permute-start.4 = (bf16[8,1,64,128]{3,2,1,0:T(8,128)(2,1)S(1)}, bf16[8,1,64,128]{3,2,1,0:T(8,128)(2,1)S(1)}, u32[]{:S(2)}, u32[]{:S(2)}) collective-permute-start(bf16[8,1,64,128]{3,2,1,0:T(8,128)(2,1)S(1)} %get-tuple-element.29), channel_id=1, source_target_pairs={{0,4},{4,8},{8,12},{12,16},{16,20},{20,24},{24,28},{28,1},{1,5},{5... | collective-permute-start | bytes 393224 | tf_op jit(solution)/shard_map/ppermute | solution.py:242
  69.0 36.6 %collective-permute-start.5 = (bf16[8,1,64,128]{3,2,1,0:T(8,128)(2,1)S(1)}, bf16[8,1,64,128]{3,2,1,0:T(8,128)(2,1)S(1)}, u32[]{:S(2)}, u32[]{:S(2)}) collective-permute-start(bf16[8,1,64,128]{3,2,1,0:T(8,128)(2,1)S(1)} %get-tuple-element.28), channel_id=1, source_target_pairs={{4,0},{8,4},{12,8},{16,12},{20,16},{24,20},{28,24},{1,28},{5,1},{9... | collective-permute-start | bytes 393224 | tf_op jit(solution)/shard_map/ppermute | solution.py:242
  70.3 0.6 copy-start.11
  71.0 0.6 copy-start.12
  79.7 8.0 %collective-permute-start.2 = (bf16[8,1,64,128]{3,2,1,0:T(8,128)(2,1)}, bf16[8,1,64,128]{3,2,1,0:T(8,128)(2,1)S(1)}, u32[]{:S(2)}, u32[]{:S(2)}) collective-permute-start(bf16[8,1,64,128]{3,2,1,0:T(8,128)(2,1)} %get-tuple-element.17), channel_id=1, source_target_pairs={{0,4},{4,8},{8,12},{12,16},{16,20},{20,24},{24,28},{28,1},{1,5},{5... | collective-permute-start | bytes 393224 | tf_op jit(solution)/shard_map/ppermute | solution.py:242
  84.2 7.1 %collective-permute-start.3 = (bf16[8,1,64,128]{3,2,1,0:T(8,128)(2,1)}, bf16[8,1,64,128]{3,2,1,0:T(8,128)(2,1)S(1)}, u32[]{:S(2)}, u32[]{:S(2)}) collective-permute-start(bf16[8,1,64,128]{3,2,1,0:T(8,128)(2,1)} %get-tuple-element.18), channel_id=1, source_target_pairs={{4,0},{8,4},{12,8},{16,12},{20,16},{24,20},{28,24},{1,28},{5,1},{9... | collective-permute-start | bytes 393224 | tf_op jit(solution)/shard_map/ppermute | solution.py:242
  87.6 3.7 %copy-start.13 = (bf16[8,1,64,128]{3,2,1,0:T(8,128)(2,1)}, bf16[8,1,64,128]{3,2,1,0:T(8,128)(2,1)S(1)}, u32[]{:S(2)}) copy-start(bf16[8,1,64,128]{3,2,1,0:T(8,128)(2,1)S(1)} %collective-permute-done.2.top_ref) | copy-start | bytes 393220
  91.3 0.6 copy-start.14
  99.1 24.2 %collective-permute-start.8 = (bf16[8,1,64,128]{3,2,1,0:T(8,128)(2,1)}, bf16[8,1,64,128]{3,2,1,0:T(8,128)(2,1)S(1)}, u32[]{:S(2)}, u32[]{:S(2)}) collective-permute-start(bf16[8,1,64,128]{3,2,1,0:T(8,128)(2,1)} %get-tuple-element.24), channel_id=1, source_target_pairs={{0,4},{4,8},{8,12},{12,16},{16,20},{20,24},{24,28},{28,1},{1,5},{5... | collective-permute-start | bytes 393224 | tf_op jit(solution)/shard_map/ppermute | solution.py:242
  102.8 20.5 %collective-permute-start.9 = (bf16[8,1,64,128]{3,2,1,0:T(8,128)(2,1)}, bf16[8,1,64,128]{3,2,1,0:T(8,128)(2,1)S(1)}, u32[]{:S(2)}, u32[]{:S(2)}) collective-permute-start(bf16[8,1,64,128]{3,2,1,0:T(8,128)(2,1)} %get-tuple-element.25), channel_id=1, source_target_pairs={{4,0},{8,4},{12,8},{16,12},{20,16},{24,20},{28,24},{1,28},{5,1},{9... | collective-permute-start | bytes 393224 | tf_op jit(solution)/shard_map/ppermute | solution.py:242
  104.5 15.9 %copy-start.4 = (bf16[3,3,64,64]{3,2,1,0:T(8,128)(2,1)S(1)}, bf16[3,3,64,64]{3,2,1,0:T(8,128)(2,1)}, u32[]{:S(2)}) copy-start(bf16[3,3,64,64]{3,2,1,0:T(8,128)(2,1)} %param.14) | copy-start | bytes 221188
  105.7 16.9 %copy-start.15 = (bf16[3,64,64]{2,1,0:T(8,128)(2,1)S(1)}, bf16[3,64,64]{2,1,0:T(8,128)(2,1)}, u32[]{:S(2)}) copy-start(bf16[3,64,64]{2,1,0:T(8,128)(2,1)} %param.16) | copy-start | bytes 73732
  105.7 0.7 copy-start.5
  105.7 0.7 copy-start.6
  106.4 31.8 %copy-start.3 = (bf16[3,3,3,64,64]{4,3,2,1,0:T(8,128)(2,1)S(1)}, bf16[3,3,3,64,64]{4,3,2,1,0:T(8,128)(2,1)}, u32[]{:S(2)}) copy-start(bf16[3,3,3,64,64]{4,3,2,1,0:T(8,128)(2,1)} %param.12) | copy-start | bytes 663556
  113.9 25.8 %collective-permute-start.6 = (bf16[8,1,64,128]{3,2,1,0:T(8,128)(2,1)}, bf16[8,1,64,128]{3,2,1,0:T(8,128)(2,1)S(1)}, u32[]{:S(2)}, u32[]{:S(2)}) collective-permute-start(bf16[8,1,64,128]{3,2,1,0:T(8,128)(2,1)} %get-tuple-element.22), channel_id=1, source_target_pairs={{0,4},{4,8},{8,12},{12,16},{16,20},{20,24},{24,28},{28,1},{1,5},{5... | collective-permute-start | bytes 393224 | tf_op jit(solution)/shard_map/ppermute | solution.py:242
  118.5 21.3 %collective-permute-start.7 = (bf16[8,1,64,128]{3,2,1,0:T(8,128)(2,1)}, bf16[8,1,64,128]{3,2,1,0:T(8,128)(2,1)S(1)}, u32[]{:S(2)}, u32[]{:S(2)}) collective-permute-start(bf16[8,1,64,128]{3,2,1,0:T(8,128)(2,1)} %get-tuple-element.23), channel_id=1, source_target_pairs={{4,0},{8,4},{12,8},{16,12},{20,16},{24,20},{28,24},{1,28},{5,1},{9... | collective-permute-start | bytes 393224 | tf_op jit(solution)/shard_map/ppermute | solution.py:242
  123.3 0.7 copy-start.7
  123.3 0.7 copy-start.9
  132.4 15.6 %all-to-all-start.4 = ((f32[8,8,128]{2,1,0:T(8,128)}), f32[8,8,128]{2,1,0:T(8,128)S(1)}, u32[]{:S(2)}, u32[]{:S(2)}) async-start(f32[8,8,128]{2,1,0:T(8,128)} %get-tuple-element.26), calls=%async_computation.4 | async-start | bytes 65536 | tf_op jit(solution)/shard_map/all_to_all | solution.py:312
  139.7 0.7 copy-start.8
  139.7 0.7 copy-start.10
  178.8 31.4 %all-to-all-start.1 = ((bf16[8,8,64,128]{3,2,1,0:T(8,128)(2,1)}), bf16[8,8,64,128]{3,2,1,0:T(8,128)(2,1)S(1)}, u32[]{:S(2)}, u32[]{:S(2)}) async-start(bf16[8,8,64,128]{3,2,1,0:T(8,128)(2,1)} %get-tuple-element.19.main_ref), calls=%async_computation.1 | async-start | bytes 2097152 | tf_op jit(solution)/shard_map/all_to_all | solution.py:283

commit v2 on v1

--- a/solution.py
+++ b/solution.py
@@ -233,13 +233,133 @@
     return kernel[::-1, ::-1, ::-1].transpose(0, 3, 1, 2, 4).reshape(a * o, b * e * c)
 
 
-def from_neighbours(first, last):
-    tiles, parts = lax.axis_size("space"), lax.axis_size("tm")
-    order = [part * tiles + tile for tile in range(tiles) for part in range(parts)]
-    up = list(zip(order[:-1], order[1:]))
-    down = [(j, i) for i, j in up]
-    names = ("tm", "space")
-    return lax.ppermute(last, names, up), lax.ppermute(first, names, down)
+def halo_kernel(first_ref, last_ref, top_ref, bottom_ref, send_sem, recv_sem):
+    parts, tiles = lax.axis_size("tm"), lax.axis_size("space")
+    place = lax.axis_index("space") * parts + lax.axis_index("tm")
+    has_before, has_after = place > 0, place < parts * tiles - 1
+    lower, upper = jnp.maximum(place - 1, 0), jnp.minimum(place + 1, parts * tiles - 1)
+    before = (lax.rem(lower, parts), lower // parts)
+    after = (lax.rem(upper, parts), upper // parts)
+
+    def move(source, target, slot, device):
+        return pltpu.make_async_remote_copy(
+            src_ref=source,
+            dst_ref=target,
+            send_sem=send_sem.at[slot],
+            recv_sem=recv_sem.at[slot],
+            device_id=device,
+            device_id_type=pl.DeviceIdType.MESH,
+        )
+
+    def down():
+        return move(first_ref, bottom_ref, 0, before)
+
+    def up():
+        return move(last_ref, top_ref, 1, after)
+
+    barrier = pltpu.get_barrier_semaphore()
+
+    @pl.when(has_before)
+    def _():
+        pl.semaphore_signal(barrier, inc=1, device_id=before, device_id_type=pl.DeviceIdType.MESH)
+
+    @pl.when(has_after)
+    def _():
+        pl.semaphore_signal(barrier, inc=1, device_id=after, device_id_type=pl.DeviceIdType.MESH)
+
+    pl.semaphore_wait(barrier, has_before.astype(jnp.int32) + has_after.astype(jnp.int32))
+
+    @pl.when(has_before)
+    def _():
+        down().start()
+
+    @pl.when(has_after)
+    def _():
+        up().start()
+
+    @pl.when(jnp.logical_not(has_before))
+    def _():
+        top_ref[...] = jnp.zeros(top_ref.shape, top_ref.dtype)
+
+    @pl.when(jnp.logical_not(has_after))
+    def _():
+        bottom_ref[...] = jnp.zeros(bottom_ref.shape, bottom_ref.dtype)
+
+    @pl.when(has_before)
+    def _():
+        down().wait_send()
+        up().wait_recv()
+
+    @pl.when(has_after)
+    def _():
+        up().wait_send()
+        down().wait_recv()
+
+
+def from_neighbours(first, last, number):
+    vmem = pl.BlockSpec(memory_space=pltpu.VMEM)
+    edge = jax.ShapeDtypeStruct(first.shape, first.dtype)
+    return pl.pallas_call(
+        halo_kernel,
+        name="halo",
+        out_shape=[edge, edge],
+        in_specs=[vmem] * 2,
+        out_specs=[vmem] * 2,
+        scratch_shapes=[pltpu.SemaphoreType.DMA((2,)), pltpu.SemaphoreType.DMA((2,))],
+        compiler_params=pltpu.CompilerParams(collective_id=number, has_side_effects=True),
+    )(first, last)
+
+
+def swap_kernel(groups, in_ref, out_ref, local_sem, send_sem, recv_sem):
+    parts = lax.axis_size("tm")
+    me, tile = lax.axis_index("tm"), lax.axis_index("space")
+    barrier = pltpu.get_barrier_semaphore()
+    for d in range(1, parts):
+        pl.semaphore_signal(
+            barrier,
+            inc=1,
+            device_id=(lax.rem(me + d, parts), tile),
+            device_id_type=pl.DeviceIdType.MESH,
+        )
+    pl.semaphore_wait(barrier, parts - 1)
+    copies = []
+    for d in range(1, parts):
+        peer = lax.rem(me + d, parts)
+        copies.append(
+            pltpu.make_async_remote_copy(
+                src_ref=in_ref.at[peer // groups],
+                dst_ref=out_ref.at[me],
+                send_sem=send_sem.at[d],
+                recv_sem=recv_sem.at[d],
+                device_id=(peer, tile),
+                device_id_type=pl.DeviceIdType.MESH,
+            )
+        )
+    for copy in copies:
+        copy.start()
+    own = pltpu.make_async_copy(in_ref.at[me // groups], out_ref.at[me], local_sem)
+    own.start()
+    own.wait()
+    for copy in copies:
+        copy.wait()
+
+
+def swap(array, number):
+    parts = lax.axis_size("tm")
+    anywhere = pl.BlockSpec(memory_space=pl.ANY)
+    return pl.pallas_call(
+        functools.partial(swap_kernel, parts // array.shape[0]),
+        name="swap",
+        out_shape=jax.ShapeDtypeStruct((parts,) + array.shape[1:], array.dtype),
+        in_specs=[anywhere],
+        out_specs=anywhere,
+        scratch_shapes=[
+            pltpu.SemaphoreType.DMA,
+            pltpu.SemaphoreType.DMA((parts,)),
+            pltpu.SemaphoreType.DMA((parts,)),
+        ],
+        compiler_params=pltpu.CompilerParams(collective_id=number, has_side_effects=True),
+    )(array)
 
 
 def shards(
@@ -258,11 +378,14 @@
     to_frames = functools.partial(lax.all_to_all, axis_name="tm", split_axis=0, concat_axis=1, tiled=True)
     tm_count = lax.axis_size("tm")
 
-    v = to_rows(video_in)
-    frames, rows, channels, width = v.shape
-    v_halo = from_neighbours(v[:, :1], v[:, rows - 1 :])
+    here, height, channels, width = video_in.shape
+    rows = height // tm_count
+    v = swap(video_in.reshape(tm_count, rows, channels, width), 0)
+    cotangent, v = lax.optimization_barrier((cotangent, v))
+    frames = here * tm_count
+    v_halo = from_neighbours(v[:, :1], v[:, rows - 1 :], 1)
     cot = to_rows(cotangent)
-    cot_halo = from_neighbours(cot[:, :1], cot[:, rows - 1 :])
+    cot_halo = from_neighbours(cot[:, :1], cot[:, rows - 1 :], 2)
 
     block = (v.shape, BF16)
     edge = ((frames, 1, channels, width), BF16)
@@ -271,18 +394,18 @@
     inner, slope, first, last = call(
         pre_kernel, [block, (v.shape, F32), edge, edge], [wide], 0, v, *v_halo, forward_weight(kernel_a)
     )
-    inner_halo = from_neighbours(first, last)
+    inner_halo = from_neighbours(first, last, 3)
     grad_pre, first, last = call(
         grad_pre_kernel, [block, edge, edge], [wide], 0, cot, *cot_halo, backward_weight(kernel_b), slope
     )
-    grad_halo = from_neighbours(first, last)
+    grad_halo = from_neighbours(first, last, 4)
     video_rows, first, last = call(
         video_kernel, [block, edge, edge], [wide], 0, inner, *inner_halo, forward_weight(kernel_b), v
     )
-    video_halo = from_neighbours(first, last)
+    video_halo = from_neighbours(first, last, 5)
     video = to_frames(video_rows)
     (grad_rows,) = call(input_grad_kernel, [block], [wide], 0, grad_pre, *grad_halo, backward_weight(kernel_a), v, cot)
-    input_grad = to_frames(grad_rows)
+    input_grad = swap(grad_rows, 6).reshape(video_in.shape)
 
     column = jnp.arange(width, dtype=jnp.int32) // 2
     pool = (column[:, None] == jnp.arange(width // 2, dtype=jnp.int32)[None, :]).astype(BF16) * 0.25
@@ -309,7 +432,7 @@
         time_head.astype(F32)[:, None],
     )
     groups = tm_count // LISTED
-    moved = lax.all_to_all(jnp.repeat(maps, groups, axis=0), "tm", split_axis=0, concat_axis=0, tiled=True)
+    moved = swap(maps, 7)
     moved = moved.reshape(groups, tm_count * rows // groups, width)
     if groups > 1:
         mine = lax.rem(lax.axis_index("tm"), groups)

time: 214 us -> 204 us (0.953)
  the two profiles are of different devices: /device:TPU:0 before, /device:TPU:14 now
where the time goes in v2:
time: 204 us
  Pallas kernels  174 us (85%)
  local copies, waits for them, and re-layouts  15.7 us (8%)
  starting transfers between devices  11.9 us (6%)
    pallas_call x5, Pallas kernels, from_neighbours(): pl.pallas_call(halo_kernel, name='halo', out_shape=[edge, edge], in_specs...  72.6 us
    pallas_call x3, Pallas kernels, swap(): pl.pallas_call(functools.partial(swap_kernel, parts // array.shape[0]), n...  62.3 us
    pallas_call x5, Pallas kernels, run(): pl.pallas_call(kernel, out_shape=[jax.ShapeDtypeStruct(shape, dtype) for...  38.9 us
    all_to_all x1, starting transfers between devices, shards(): cot = to_rows(cotangent)  6.08 us
    all_to_all x1, starting transfers between devices, shards(): video = to_frames(video_rows)  5.78 us
  transfers between devices with their start and end apart: 2, of which 0 were waited for; matrix products, arithmetic and copies ran while one was open for 7% of the time, Pallas kernels for 72%

profile of v2, /device:TPU:14, one launch (start us, length us, event | category | flops | bytes accessed | tf_op | source)
XLA Modules:
  0.0 203.6 jit_solution(11076266781867951109)
XLA Ops:
  0.6 0.0 copy-start.3
  0.6 27.5 %swap.3.main_ref.in_ref = bf16[8,8,64,128]{3,2,1,0:T(8,128)(2,1)} custom-call(bf16[8,8,64,128]{3,2,1,0:T(8,128)(2,1)} %bitcast.32), custom_call_target="tpu_custom_call" | custom-call | tf_op jit(solution)/shard_map/swap/pallas_call | solution.py:350
  28.1 0.0 copy-start.2
  28.1 6.1 %all-to-all-start.1 = ((bf16[1,64,64,128]{3,2,0,1:T(8,128)(2,1)}), bf16[1,64,64,128]{3,2,0,1:T(8,128)(2,1)S(1)}, u32[]{:S(2)}, u32[]{:S(2)}) async-start(bf16[1,64,64,128]{3,2,0,1:T(8,128)(2,1)} %bitcast.4), calls=%async_computation.1 | async-start | bytes 2097152 | tf_op jit(solution)/shard_map/all_to_all | solution.py:387
  34.2 0.0 copy-done.3
  34.2 0.9 copy.32
  35.2 1.1 reshape.55.weight_ref
  36.3 0.0 copy-done.2
  36.3 0.9 copy.33
  37.2 1.1 reshape.56.weight_ref
  38.3 1.7 fusion.2
  40.0 21.5 %halo.5 = (bf16[8,1,64,128]{3,2,1,0:T(8,128)(2,1)}, bf16[8,1,64,128]{3,2,1,0:T(8,128)(2,1)}) custom-call(bf16[8,1,64,128]{3,2,1,0:T(8,128)(2,1)} %get-tuple-element.55.first_ref, bf16[8,1,64,128]{3,2,1,0:T(8,128)(2,1)} %get-tuple-element.54.last_ref), custom_call_target="tpu_custom_call" | custom-call | tf_op jit(solution)/shard_map/halo/pallas_call | solution.py:302
  61.4 8.0 %shard_map.129 = (bf16[8,8,64,128]{3,2,1,0:T(8,128)(2,1)}, f32[8,8,64,128]{3,2,1,0:T(8,128)}, bf16[8,1,64,128]{3,2,1,0:T(8,128)(2,1)}, bf16[8,1,64,128]{3,2,1,0:T(8,128)(2,1)}) custom-call(bf16[8,8,64,128]{3,2,1,0:T(8,128)(2,1)} %swap.3.main_ref.in_ref, bf16[8,1,64,128]{3,2,1,0:T(8,128)(2,1)} %get-tuple-element.29.top_ref, ...), custom_call_target="tpu_custom_call" | custom-call | tf_op jit(solution)/shard_map/pallas_call | solution.py:216
  69.5 8.1 %halo.6 = (bf16[8,1,64,128]{3,2,1,0:T(8,128)(2,1)}, bf16[8,1,64,128]{3,2,1,0:T(8,128)(2,1)}) custom-call(bf16[8,1,64,128]{3,2,1,0:T(8,128)(2,1)} %get-tuple-element.32.first_ref, bf16[8,1,64,128]{3,2,1,0:T(8,128)(2,1)} %get-tuple-element.33.last_ref), custom_call_target="tpu_custom_call" | custom-call | tf_op jit(solution)/shard_map/halo/pallas_call | solution.py:302
  77.5 0.0 copy-start.4
  77.6 0.0 copy-start.7
  77.6 0.0 copy-start.8
  77.6 0.0 copy-start.9
  77.6 0.0 copy-start.6
  77.6 7.2 %shard_map.130 = (bf16[8,8,64,128]{3,2,1,0:T(8,128)(2,1)}, bf16[8,1,64,128]{3,2,1,0:T(8,128)(2,1)}, bf16[8,1,64,128]{3,2,1,0:T(8,128)(2,1)}) custom-call(bf16[8,8,64,128]{3,2,1,0:T(8,128)(2,1)} %get-tuple-element.31.main_ref, bf16[8,1,64,128]{3,2,1,0:T(8,128)(2,1)} %get-tuple-element.34.top_ref, bf16[8,1,64,128]{3,2,1,0:T(8,128)(2,1)} %get-tuple-element.35.bottom_ref, ...), custom_call_target="tpu_custom_call" | custom-call | tf_op jit(solution)/shard_map/pallas_call | solution.py:216
  84.8 0.0 all-to-all-done.1
  84.8 0.0 copy-start
  84.8 5.8 %all-to-all-start = ((bf16[8,8,64,128]{3,2,1,0:T(8,128)(2,1)}), bf16[8,8,64,128]{3,2,1,0:T(8,128)(2,1)S(1)}, u32[]{:S(2)}, u32[]{:S(2)}) async-start(bf16[8,8,64,128]{3,2,1,0:T(8,128)(2,1)} %get-tuple-element.36.main_ref), calls=%async_computation | async-start | bytes 2097152 | tf_op jit(solution)/shard_map/all_to_all | solution.py:406
  90.6 0.0 copy-done.4
  90.6 0.8 copy.37
  91.3 0.0 copy-done.7
  91.3 0.1 copy.39
  91.4 0.0 copy-done.8
  91.5 0.7 copy.40.plane_head_ref
  92.2 0.0 copy-done.9
  92.2 0.7 copy.41.time_head_ref
  92.9 0.0 copy-done.6
  92.9 0.7 copy.38
  93.6 24.4 %halo.9 = (bf16[8,1,64,128]{3,2,1,0:T(8,128)(2,1)}, bf16[8,1,64,128]{3,2,1,0:T(8,128)(2,1)}) custom-call(bf16[8,1,64,128]{3,2,1,0:T(8,128)(2,1)} %get-tuple-element.46.first_ref, bf16[8,1,64,128]{3,2,1,0:T(8,128)(2,1)} %get-tuple-element.47.last_ref), custom_call_target="tpu_custom_call" | custom-call | tf_op jit(solution)/shard_map/halo/pallas_call | solution.py:302
  118.0 0.1 fusion
  118.1 0.6 pad_maximum_fusion.pool_ref
  118.7 0.6 convert_bitcast_fusion.mixer_ref
  119.3 8.5 %shard_map.133 = (f32[8,8,128]{2,1,0:T(8,128)}, f32[4,1,64]{2,1,0:T(1,128)}) custom-call(s32[8]{0:T(128)} %listed_ref.1, bf16[8,8,64,128]{3,2,1,0:T(8,128)(2,1)} %get-tuple-element.36.main_ref, bf16[8,1,64,128]{3,2,1,0:T(8,128)(2,1)} %get-tuple-element.48.top_ref, bf16[8,1,64,128]{3,2,1,0:T(8,128)(2,1)} %get-tuple-element.49.bottom_ref, ...), custom_call_target="tpu_custom_call" | custom-call | tf_op jit(solution)/shard_map/pallas_call | solution.py:216
  127.8 6.0 %swap.5 = f32[8,8,128]{2,1,0:T(8,128)} custom-call(f32[8,8,128]{2,1,0:T(8,128)} %get-tuple-element.50.in_ref), custom_call_target="tpu_custom_call" | custom-call | tf_op jit(solution)/shard_map/swap/pallas_call | solution.py:350
  133.8 0.4 copy.35
  134.2 1.1 reshape.57.weight_ref
  135.4 0.4 copy.36
  135.8 1.1 reshape.58.weight_ref
  136.9 0.0 copy-done
  136.9 0.7 fusion.1
  137.6 8.9 %halo.7 = (bf16[8,1,64,128]{3,2,1,0:T(8,128)(2,1)}, bf16[8,1,64,128]{3,2,1,0:T(8,128)(2,1)}) custom-call(bf16[8,1,64,128]{3,2,1,0:T(8,128)(2,1)} %get-tuple-element.53.first_ref, bf16[8,1,64,128]{3,2,1,0:T(8,128)(2,1)} %get-tuple-element.52.last_ref), custom_call_target="tpu_custom_call" | custom-call | tf_op jit(solution)/shard_map/halo/pallas_call | solution.py:302
  146.5 7.6 %shard_map.131 = (bf16[8,8,64,128]{3,2,1,0:T(8,128)(2,1)}, bf16[8,1,64,128]{3,2,1,0:T(8,128)(2,1)}, bf16[8,1,64,128]{3,2,1,0:T(8,128)(2,1)}) custom-call(bf16[8,8,64,128]{3,2,1,0:T(8,128)(2,1)} %bitcast.26, bf16[8,1,64,128]{3,2,1,0:T(8,128)(2,1)} %get-tuple-element.38.top_ref, bf16[8,1,64,128]{3,2,1,0:T(8,128)(2,1)} %get-tuple-element.39.bottom_ref, ...), custom_call_target="tpu_custom_call" | custom-call | tf_op jit(solution)/shard_map/pallas_call | solution.py:216
  154.1 9.8 %halo.8 = (bf16[8,1,64,128]{3,2,1,0:T(8,128)(2,1)}, bf16[8,1,64,128]{3,2,1,0:T(8,128)(2,1)}) custom-call(bf16[8,1,64,128]{3,2,1,0:T(8,128)(2,1)} %get-tuple-element.42.first_ref, bf16[8,1,64,128]{3,2,1,0:T(8,128)(2,1)} %get-tuple-element.43.last_ref), custom_call_target="tpu_custom_call" | custom-call | tf_op jit(solution)/shard_map/halo/pallas_call | solution.py:302
  163.9 7.6 %shard_map.132.in_ref = bf16[8,8,64,128]{3,2,1,0:T(8,128)(2,1)} custom-call(bf16[8,8,64,128]{3,2,1,0:T(8,128)(2,1)} %get-tuple-element.41.main_ref, bf16[8,1,64,128]{3,2,1,0:T(8,128)(2,1)} %get-tuple-element.44.top_ref, bf16[8,1,64,128]{3,2,1,0:T(8,128)(2,1)} %get-tuple-element.45.bottom_ref, bf16[192,576]{1,0:T(8,128)(2,1)} %reshape.58.weight_ref, ...), custom_call_target="tpu_custom_call" | custom-call | tf_op jit(solution)/shard_map/pallas_call | solution.py:216
  171.5 28.8 %swap.4 = bf16[8,8,64,128]{3,2,1,0:T(8,128)(2,1)} custom-call(bf16[8,8,64,128]{3,2,1,0:T(8,128)(2,1)} %shard_map.132.in_ref), custom_call_target="tpu_custom_call" | custom-call | tf_op jit(solution)/shard_map/swap/pallas_call | solution.py:350
  200.4 0.0 copy-start.1
  200.4 0.0 all-to-all-done
  200.4 0.0 copy-start.5
  200.4 1.0 copy.45
  201.4 0.6 copy-done.1
  202.0 1.0 copy.46
  202.9 0.0 copy-done.5
  202.9 0.6 copy.47
  (5 shorter events, 0.1 us)
Async XLA Ops:
  0.6 33.6 %copy-start.3 = (bf16[3,3,3,64,64]{4,3,2,1,0:T(8,128)(2,1)S(1)}, bf16[3,3,3,64,64]{4,3,2,1,0:T(8,128)(2,1)}, u32[]{:S(2)}) copy-start(bf16[3,3,3,64,64]{4,3,2,1,0:T(8,128)(2,1)} %param.12) | copy-start | bytes 663556
  28.1 8.1 %copy-start.2 = (bf16[3,3,3,64,64]{4,3,2,1,0:T(8,128)(2,1)S(1)}, bf16[3,3,3,64,64]{4,3,2,1,0:T(8,128)(2,1)}, u32[]{:S(2)}) copy-start(bf16[3,3,3,64,64]{4,3,2,1,0:T(8,128)(2,1)} %param.13) | copy-start | bytes 663556
  28.1 56.6 %all-to-all-start.1 = ((bf16[1,64,64,128]{3,2,0,1:T(8,128)(2,1)}), bf16[1,64,64,128]{3,2,0,1:T(8,128)(2,1)S(1)}, u32[]{:S(2)}, u32[]{:S(2)}) async-start(bf16[1,64,64,128]{3,2,0,1:T(8,128)(2,1)} %bitcast.4), calls=%async_computation.1 | async-start | bytes 2097152 | tf_op jit(solution)/shard_map/all_to_all | solution.py:387
  77.5 13.0 %copy-start.4 = (bf16[3,3,64,64]{3,2,1,0:T(8,128)(2,1)S(1)}, bf16[3,3,64,64]{3,2,1,0:T(8,128)(2,1)}, u32[]{:S(2)}) copy-start(bf16[3,3,64,64]{3,2,1,0:T(8,128)(2,1)} %param.14) | copy-start | bytes 221188
  77.6 13.8 %copy-start.7 = (bf16[64,64]{1,0:T(8,128)(2,1)S(1)}, bf16[64,64]{1,0:T(8,128)(2,1)}, u32[]{:S(2)}) copy-start(bf16[64,64]{1,0:T(8,128)(2,1)} %param.17) | copy-start | bytes 24580
  77.6 13.9 %copy-start.8 = (bf16[64]{0:T(256)(128)(2,1)S(1)}, bf16[64]{0:T(256)(128)(2,1)}, u32[]{:S(2)}) copy-start(bf16[64]{0:T(256)(128)(2,1)} %param.15) | copy-start | bytes 388
  77.6 14.6 %copy-start.9 = (bf16[64]{0:T(256)(128)(2,1)S(1)}, bf16[64]{0:T(256)(128)(2,1)}, u32[]{:S(2)}) copy-start(bf16[64]{0:T(256)(128)(2,1)} %param.18) | copy-start | bytes 388
  77.6 15.3 %copy-start.6 = (bf16[3,64,64]{2,1,0:T(8,128)(2,1)S(1)}, bf16[3,64,64]{2,1,0:T(8,128)(2,1)}, u32[]{:S(2)}) copy-start(bf16[3,64,64]{2,1,0:T(8,128)(2,1)} %param.16) | copy-start | bytes 73732
  84.8 52.1 %copy-start = (bf16[1,64,64,128]{3,2,0,1:T(8,128)(2,1)}, bf16[1,64,64,128]{3,2,0,1:T(8,128)(2,1)S(1)}, u32[]{:S(2)}) copy-start(bf16[1,64,64,128]{3,2,0,1:T(8,128)(2,1)S(1)} %all-to-all-done.1) | copy-start | bytes 3145732
  84.8 115.6 %all-to-all-start = ((bf16[8,8,64,128]{3,2,1,0:T(8,128)(2,1)}), bf16[8,8,64,128]{3,2,1,0:T(8,128)(2,1)S(1)}, u32[]{:S(2)}, u32[]{:S(2)}) async-start(bf16[8,8,64,128]{3,2,1,0:T(8,128)(2,1)} %get-tuple-element.36.main_ref), calls=%async_computation | async-start | bytes 2097152 | tf_op jit(solution)/shard_map/all_to_all | solution.py:406
  200.4 1.6 copy-start.1
  200.4 2.6 %copy-start.5 = (f32[8,8,128]{2,1,0:T(8,128)S(1)}, f32[8,8,128]{2,1,0:T(8,128)}, u32[]{:S(2)}) copy-start(f32[8,8,128]{2,1,0:T(8,128)} %swap.5) | copy-start | bytes 98308

commit v3 on v2

--- a/solution.py
+++ b/solution.py
@@ -310,7 +310,10 @@
     )(first, last)
 
 
-def swap_kernel(groups, in_ref, out_ref, local_sem, send_sem, recv_sem):
+def swap_kernel(groups, *refs):
+    count = len(groups)
+    pairs = list(zip(groups, refs[:count], refs[count : 2 * count]))
+    local_sem, send_sem, recv_sem = refs[2 * count :]
     parts = lax.axis_size("tm")
     me, tile = lax.axis_index("tm"), lax.axis_index("space")
     barrier = pltpu.get_barrier_semaphore()
@@ -323,43 +326,44 @@
         )
     pl.semaphore_wait(barrier, parts - 1)
     copies = []
-    for d in range(1, parts):
-        peer = lax.rem(me + d, parts)
-        copies.append(
-            pltpu.make_async_remote_copy(
-                src_ref=in_ref.at[peer // groups],
-                dst_ref=out_ref.at[me],
-                send_sem=send_sem.at[d],
-                recv_sem=recv_sem.at[d],
-                device_id=(peer, tile),
-                device_id_type=pl.DeviceIdType.MESH,
+    for n, (group, in_ref, out_ref) in enumerate(pairs):
+        for d in range(1, parts):
+            peer = lax.rem(me + d, parts)
+            copies.append(
+                pltpu.make_async_remote_copy(
+                    src_ref=in_ref.at[peer // group],
+                    dst_ref=out_ref.at[me],
+                    send_sem=send_sem.at[n, d],
+                    recv_sem=recv_sem.at[n, d],
+                    device_id=(peer, tile),
+                    device_id_type=pl.DeviceIdType.MESH,
+                )
             )
-        )
+    for n, (group, in_ref, out_ref) in enumerate(pairs):
+        copies.append(pltpu.make_async_copy(in_ref.at[me // group], out_ref.at[me], local_sem.at[n]))
     for copy in copies:
         copy.start()
-    own = pltpu.make_async_copy(in_ref.at[me // groups], out_ref.at[me], local_sem)
-    own.start()
-    own.wait()
     for copy in copies:
         copy.wait()
 
 
-def swap(array, number):
+def swap(number, *arrays):
     parts = lax.axis_size("tm")
     anywhere = pl.BlockSpec(memory_space=pl.ANY)
+    count = len(arrays)
     return pl.pallas_call(
-        functools.partial(swap_kernel, parts // array.shape[0]),
+        functools.partial(swap_kernel, [parts // array.shape[0] for array in arrays]),
         name="swap",
-        out_shape=jax.ShapeDtypeStruct((parts,) + array.shape[1:], array.dtype),
-        in_specs=[anywhere],
-        out_specs=anywhere,
+        out_shape=[jax.ShapeDtypeStruct((parts,) + array.shape[1:], array.dtype) for array in arrays],
+        in_specs=[anywhere] * count,
+        out_specs=[anywhere] * count,
         scratch_shapes=[
-            pltpu.SemaphoreType.DMA,
-            pltpu.SemaphoreType.DMA((parts,)),
-            pltpu.SemaphoreType.DMA((parts,)),
+            pltpu.SemaphoreType.DMA((count,)),
+            pltpu.SemaphoreType.DMA((count, parts)),
+            pltpu.SemaphoreType.DMA((count, parts)),
         ],
         compiler_params=pltpu.CompilerParams(collective_id=number, has_side_effects=True),
-    )(array)
+    )(*arrays)
 
 
 def shards(
@@ -380,7 +384,7 @@
 
     here, height, channels, width = video_in.shape
     rows = height // tm_count
-    v = swap(video_in.reshape(tm_count, rows, channels, width), 0)
+    (v,) = swap(0, video_in.reshape(tm_count, rows, channels, width))
     cotangent, v = lax.optimization_barrier((cotangent, v))
     frames = here * tm_count
     v_halo = from_neighbours(v[:, :1], v[:, rows - 1 :], 1)
@@ -405,7 +409,6 @@
     video_halo = from_neighbours(first, last, 5)
     video = to_frames(video_rows)
     (grad_rows,) = call(input_grad_kernel, [block], [wide], 0, grad_pre, *grad_halo, backward_weight(kernel_a), v, cot)
-    input_grad = swap(grad_rows, 6).reshape(video_in.shape)
 
     column = jnp.arange(width, dtype=jnp.int32) // 2
     pool = (column[:, None] == jnp.arange(width // 2, dtype=jnp.int32)[None, :]).astype(BF16) * 0.25
@@ -432,7 +435,8 @@
         time_head.astype(F32)[:, None],
     )
     groups = tm_count // LISTED
-    moved = swap(maps, 7)
+    input_grad, moved = swap(6, grad_rows, maps)
+    input_grad = input_grad.reshape(video_in.shape)
     moved = moved.reshape(groups, tm_count * rows // groups, width)
     if groups > 1:
         mine = lax.rem(lax.axis_index("tm"), groups)

time: 204 us -> 195 us (0.956)
  the two profiles are of different devices: /device:TPU:14 before, /device:TPU:0 now
where the time goes in v3:
time: 195 us
  Pallas kernels  155 us (79%)
  starting transfers between devices  21.9 us (11%)
  local copies, waits for them, and re-layouts  15.7 us (8%)
    pallas_call x5, Pallas kernels, from_neighbours(): pl.pallas_call(halo_kernel, name='halo', out_shape=[edge, edge], in_specs...  62.5 us
    pallas_call x2, Pallas kernels, swap(): pl.pallas_call(functools.partial(swap_kernel, [parts // array.shape[0] fo...  53.7 us
    pallas_call x5, Pallas kernels, run(): pl.pallas_call(kernel, out_shape=[jax.ShapeDtypeStruct(shape, dtype) for...  38.9 us
    all_to_all x1, starting transfers between devices, shards(): cot = to_rows(cotangent)  11.3 us
    all_to_all x1, starting transfers between devices, shards(): video = to_frames(video_rows)  10.6 us
  transfers between devices with their start and end apart: 2, of which 0 were waited for; matrix products, arithmetic and copies ran while one was open for 7% of the time, Pallas kernels for 68%

profile of v3, /device:TPU:0, one launch (start us, length us, event | category | flops | bytes accessed | tf_op | source)
XLA Modules:
  0.0 194.8 jit_solution(2936759647832324863)
XLA Ops:
  0.6 0.0 copy-start.2
  0.6 23.4 %swap.2.main_ref.in_ref = bf16[8,8,64,128]{3,2,1,0:T(8,128)(2,1)} custom-call(bf16[8,8,64,128]{3,2,1,0:T(8,128)(2,1)} %bitcast.31), custom_call_target="tpu_custom_call" | custom-call | tf_op jit(solution)/shard_map/swap/pallas_call | solution.py:354
  24.0 0.0 copy-start.1
  24.0 11.3 %all-to-all-start.1 = ((bf16[1,64,64,128]{3,2,0,1:T(8,128)(2,1)}), bf16[1,64,64,128]{3,2,0,1:T(8,128)(2,1)S(1)}, u32[]{:S(2)}, u32[]{:S(2)}) async-start(bf16[1,64,64,128]{3,2,0,1:T(8,128)(2,1)} %bitcast.4), calls=%async_computation.1 | async-start | bytes 2097152 | tf_op jit(solution)/shard_map/all_to_all | solution.py:391
  35.3 0.0 copy-done.2
  35.3 0.9 copy.32
  36.3 1.1 reshape.55.weight_ref
  37.4 0.0 copy-done.1
  37.4 0.9 copy.33
  38.3 1.1 reshape.56.weight_ref
  39.4 1.7 fusion.2
  41.1 10.1 %halo.5 = (bf16[8,1,64,128]{3,2,1,0:T(8,128)(2,1)}, bf16[8,1,64,128]{3,2,1,0:T(8,128)(2,1)}) custom-call(bf16[8,1,64,128]{3,2,1,0:T(8,128)(2,1)} %get-tuple-element.59.first_ref, bf16[8,1,64,128]{3,2,1,0:T(8,128)(2,1)} %get-tuple-element.58.last_ref), custom_call_target="tpu_custom_call" | custom-call | tf_op jit(solution)/shard_map/halo/pallas_call | solution.py:302
  51.2 8.1 %shard_map.129 = (bf16[8,8,64,128]{3,2,1,0:T(8,128)(2,1)}, f32[8,8,64,128]{3,2,1,0:T(8,128)}, bf16[8,1,64,128]{3,2,1,0:T(8,128)(2,1)}, bf16[8,1,64,128]{3,2,1,0:T(8,128)(2,1)}) custom-call(bf16[8,8,64,128]{3,2,1,0:T(8,128)(2,1)} %swap.2.main_ref.in_ref, bf16[8,1,64,128]{3,2,1,0:T(8,128)(2,1)} %get-tuple-element.31.top_ref, ...), custom_call_target="tpu_custom_call" | custom-call | tf_op jit(solution)/shard_map/pallas_call | solution.py:216
  59.2 14.7 %halo.6 = (bf16[8,1,64,128]{3,2,1,0:T(8,128)(2,1)}, bf16[8,1,64,128]{3,2,1,0:T(8,128)(2,1)}) custom-call(bf16[8,1,64,128]{3,2,1,0:T(8,128)(2,1)} %get-tuple-element.34.first_ref, bf16[8,1,64,128]{3,2,1,0:T(8,128)(2,1)} %get-tuple-element.35.last_ref), custom_call_target="tpu_custom_call" | custom-call | tf_op jit(solution)/shard_map/halo/pallas_call | solution.py:302
  73.9 0.0 copy-start.4
  73.9 0.0 copy-start.7
  73.9 0.0 copy-start.8
  73.9 0.0 copy-start.9
  74.0 0.0 copy-start.5
  74.0 7.2 %shard_map.130 = (bf16[8,8,64,128]{3,2,1,0:T(8,128)(2,1)}, bf16[8,1,64,128]{3,2,1,0:T(8,128)(2,1)}, bf16[8,1,64,128]{3,2,1,0:T(8,128)(2,1)}) custom-call(bf16[8,8,64,128]{3,2,1,0:T(8,128)(2,1)} %get-tuple-element.33.main_ref, bf16[8,1,64,128]{3,2,1,0:T(8,128)(2,1)} %get-tuple-element.36.top_ref, bf16[8,1,64,128]{3,2,1,0:T(8,128)(2,1)} %get-tuple-element.37.bottom_ref, ...), custom_call_target="tpu_custom_call" | custom-call | tf_op jit(solution)/shard_map/pallas_call | solution.py:216
  81.2 0.0 all-to-all-done.1
  81.2 0.0 copy-start
  81.2 10.6 %all-to-all-start = ((bf16[8,8,64,128]{3,2,1,0:T(8,128)(2,1)}), bf16[8,8,64,128]{3,2,1,0:T(8,128)(2,1)S(1)}, u32[]{:S(2)}, u32[]{:S(2)}) async-start(bf16[8,8,64,128]{3,2,1,0:T(8,128)(2,1)} %get-tuple-element.38.main_ref), calls=%async_computation | async-start | bytes 2097152 | tf_op jit(solution)/shard_map/all_to_all | solution.py:410
  91.7 0.0 copy-done.4
  91.7 0.8 copy.37
  92.5 0.0 copy-done.7
  92.5 0.1 copy.39
  92.6 0.0 copy-done.8
  92.6 0.7 copy.40.plane_head_ref
  93.3 0.0 copy-done.9
  93.3 0.7 copy.41.time_head_ref
  94.0 0.0 copy-done.5
  94.0 0.7 copy.38
  94.8 0.4 copy.35
  95.2 1.1 reshape.57.weight_ref
  96.3 0.4 copy.36
  96.7 1.1 reshape.58.weight_ref
  97.8 10.2 %halo.9 = (bf16[8,1,64,128]{3,2,1,0:T(8,128)(2,1)}, bf16[8,1,64,128]{3,2,1,0:T(8,128)(2,1)}) custom-call(bf16[8,1,64,128]{3,2,1,0:T(8,128)(2,1)} %get-tuple-element.48.first_ref, bf16[8,1,64,128]{3,2,1,0:T(8,128)(2,1)} %get-tuple-element.49.last_ref), custom_call_target="tpu_custom_call" | custom-call | tf_op jit(solution)/shard_map/halo/pallas_call | solution.py:302
  108.1 0.1 fusion
  108.2 0.6 pad_maximum_fusion.pool_ref
  108.8 0.6 convert_bitcast_fusion.mixer_ref
  109.4 8.4 %shard_map.133 = (f32[8,8,128]{2,1,0:T(8,128)}, f32[4,1,64]{2,1,0:T(1,128)}) custom-call(s32[8]{0:T(128)} %listed_ref.1, bf16[8,8,64,128]{3,2,1,0:T(8,128)(2,1)} %get-tuple-element.38.main_ref, bf16[8,1,64,128]{3,2,1,0:T(8,128)(2,1)} %get-tuple-element.50.top_ref, bf16[8,1,64,128]{3,2,1,0:T(8,128)(2,1)} %get-tuple-element.51.bottom_ref, ...), custom_call_target="tpu_custom_call" | custom-call | tf_op jit(solution)/shard_map/pallas_call | solution.py:216
  117.9 0.0 copy-done
  117.9 0.7 fusion.1
  118.6 14.2 %halo.7 = (bf16[8,1,64,128]{3,2,1,0:T(8,128)(2,1)}, bf16[8,1,64,128]{3,2,1,0:T(8,128)(2,1)}) custom-call(bf16[8,1,64,128]{3,2,1,0:T(8,128)(2,1)} %get-tuple-element.57.first_ref, bf16[8,1,64,128]{3,2,1,0:T(8,128)(2,1)} %get-tuple-element.56.last_ref), custom_call_target="tpu_custom_call" | custom-call | tf_op jit(solution)/shard_map/halo/pallas_call | solution.py:302
  132.8 7.5 %shard_map.131 = (bf16[8,8,64,128]{3,2,1,0:T(8,128)(2,1)}, bf16[8,1,64,128]{3,2,1,0:T(8,128)(2,1)}, bf16[8,1,64,128]{3,2,1,0:T(8,128)(2,1)}) custom-call(bf16[8,8,64,128]{3,2,1,0:T(8,128)(2,1)} %bitcast.26, bf16[8,1,64,128]{3,2,1,0:T(8,128)(2,1)} %get-tuple-element.40.top_ref, bf16[8,1,64,128]{3,2,1,0:T(8,128)(2,1)} %get-tuple-element.41.bottom_ref, ...), custom_call_target="tpu_custom_call" | custom-call | tf_op jit(solution)/shard_map/pallas_call | solution.py:216
  140.3 13.3 %halo.8 = (bf16[8,1,64,128]{3,2,1,0:T(8,128)(2,1)}, bf16[8,1,64,128]{3,2,1,0:T(8,128)(2,1)}) custom-call(bf16[8,1,64,128]{3,2,1,0:T(8,128)(2,1)} %get-tuple-element.44.first_ref, bf16[8,1,64,128]{3,2,1,0:T(8,128)(2,1)} %get-tuple-element.45.last_ref), custom_call_target="tpu_custom_call" | custom-call | tf_op jit(solution)/shard_map/halo/pallas_call | solution.py:302
  153.6 7.6 %shard_map.132.refs_0_ = bf16[8,8,64,128]{3,2,1,0:T(8,128)(2,1)} custom-call(bf16[8,8,64,128]{3,2,1,0:T(8,128)(2,1)} %get-tuple-element.43.main_ref, bf16[8,1,64,128]{3,2,1,0:T(8,128)(2,1)} %get-tuple-element.46.top_ref, bf16[8,1,64,128]{3,2,1,0:T(8,128)(2,1)} %get-tuple-element.47.bottom_ref, bf16[192,576]{1,0:T(8,128)(2,1)} %reshape.58.weight_ref, ...), custom_call_target="tpu_custom_call" | custom-call | tf_op jit(solution)/shard_map/pallas_call | solution.py:216
  161.3 30.4 %swap.3 = (bf16[8,8,64,128]{3,2,1,0:T(8,128)(2,1)}, f32[8,8,128]{2,1,0:T(8,128)}) custom-call(bf16[8,8,64,128]{3,2,1,0:T(8,128)(2,1)} %shard_map.132.refs_0_, f32[8,8,128]{2,1,0:T(8,128)} %get-tuple-element.52.refs_1_), custom_call_target="tpu_custom_call" | custom-call | tf_op jit(solution)/shard_map/swap/pallas_call | solution.py:354
  191.6 0.0 copy-start.3
  191.6 0.0 all-to-all-done
  191.7 0.0 copy-start.6
  191.7 1.0 copy.45
  192.6 0.6 copy-done.3
  193.2 1.0 copy.46
  194.2 0.0 copy-done.6
  194.2 0.6 copy.47
  (5 shorter events, 0.1 us)
Async XLA Ops:
  0.6 34.7 %copy-start.2 = (bf16[3,3,3,64,64]{4,3,2,1,0:T(8,128)(2,1)S(1)}, bf16[3,3,3,64,64]{4,3,2,1,0:T(8,128)(2,1)}, u32[]{:S(2)}) copy-start(bf16[3,3,3,64,64]{4,3,2,1,0:T(8,128)(2,1)} %param.12) | copy-start | bytes 663556
  24.0 13.3 %copy-start.1 = (bf16[3,3,3,64,64]{4,3,2,1,0:T(8,128)(2,1)S(1)}, bf16[3,3,3,64,64]{4,3,2,1,0:T(8,128)(2,1)}, u32[]{:S(2)}) copy-start(bf16[3,3,3,64,64]{4,3,2,1,0:T(8,128)(2,1)} %param.13) | copy-start | bytes 663556
  24.0 57.1 %all-to-all-start.1 = ((bf16[1,64,64,128]{3,2,0,1:T(8,128)(2,1)}), bf16[1,64,64,128]{3,2,0,1:T(8,128)(2,1)S(1)}, u32[]{:S(2)}, u32[]{:S(2)}) async-start(bf16[1,64,64,128]{3,2,0,1:T(8,128)(2,1)} %bitcast.4), calls=%async_computation.1 | async-start | bytes 2097152 | tf_op jit(solution)/shard_map/all_to_all | solution.py:391
  73.9 17.8 %copy-start.4 = (bf16[3,3,64,64]{3,2,1,0:T(8,128)(2,1)S(1)}, bf16[3,3,64,64]{3,2,1,0:T(8,128)(2,1)}, u32[]{:S(2)}) copy-start(bf16[3,3,64,64]{3,2,1,0:T(8,128)(2,1)} %param.14) | copy-start | bytes 221188
  73.9 18.6 %copy-start.7 = (bf16[64,64]{1,0:T(8,128)(2,1)S(1)}, bf16[64,64]{1,0:T(8,128)(2,1)}, u32[]{:S(2)}) copy-start(bf16[64,64]{1,0:T(8,128)(2,1)} %param.17) | copy-start | bytes 24580
  73.9 18.6 %copy-start.8 = (bf16[64]{0:T(256)(128)(2,1)S(1)}, bf16[64]{0:T(256)(128)(2,1)}, u32[]{:S(2)}) copy-start(bf16[64]{0:T(256)(128)(2,1)} %param.15) | copy-start | bytes 388
  73.9 19.4 %copy-start.9 = (bf16[64]{0:T(256)(128)(2,1)S(1)}, bf16[64]{0:T(256)(128)(2,1)}, u32[]{:S(2)}) copy-start(bf16[64]{0:T(256)(128)(2,1)} %param.18) | copy-start | bytes 388
  74.0 20.1 %copy-start.5 = (bf16[3,64,64]{2,1,0:T(8,128)(2,1)S(1)}, bf16[3,64,64]{2,1,0:T(8,128)(2,1)}, u32[]{:S(2)}) copy-start(bf16[3,64,64]{2,1,0:T(8,128)(2,1)} %param.16) | copy-start | bytes 73732
  81.2 36.7 %copy-start = (bf16[1,64,64,128]{3,2,0,1:T(8,128)(2,1)}, bf16[1,64,64,128]{3,2,0,1:T(8,128)(2,1)S(1)}, u32[]{:S(2)}) copy-start(bf16[1,64,64,128]{3,2,0,1:T(8,128)(2,1)S(1)} %all-to-all-done.1) | copy-start | bytes 3145732
  81.2 110.5 %all-to-all-start = ((bf16[8,8,64,128]{3,2,1,0:T(8,128)(2,1)}), bf16[8,8,64,128]{3,2,1,0:T(8,128)(2,1)S(1)}, u32[]{:S(2)}, u32[]{:S(2)}) async-start(bf16[8,8,64,128]{3,2,1,0:T(8,128)(2,1)} %get-tuple-element.38.main_ref), calls=%async_computation | async-start | bytes 2097152 | tf_op jit(solution)/shard_map/all_to_all | solution.py:410
  191.6 1.6 copy-start.3
  191.7 2.6 %copy-start.6 = (f32[8,8,128]{2,1,0:T(8,128)S(1)}, f32[8,8,128]{2,1,0:T(8,128)}, u32[]{:S(2)}) copy-start(f32[8,8,128]{2,1,0:T(8,128)} %get-tuple-element.54) | copy-start | bytes 98308
